TPU v7x, 256 devices: a whole 4x4x8 slice. The times are simulated.
256 devices in a mesh: depth: 2 (over core), tile: 128 (over z, y, x).
Axes of the slice: x: 4, y: 4, z: 8, core: 2. Of those that a mesh axis runs over, the one named last changes fastest.
Arguments:
- object_layer_slices: float32 [2, 16384, 2, 2048], P('depth', 'tile'), may hold values from 0.2 to 1
- probe_wave: bfloat16 [256, 2, 256], replicated, may hold values from -5 to 5
- propagator: bfloat16 [256, 2, 256], replicated, may hold values from -0.25 to 0.25
- positions: int32 [128, 2, 5, 2], P('tile'), may hold values from 0 to 1792, as said below
- counts: int32 [128, 2], P('tile'), may hold values from 2 to 5
- measured: float32 [128, 2, 5, 256, 256], P('tile'), may hold values from 0 to 2
Outputs:
- object_gradient: float32 [2, 16384, 2, 2048], P('depth', 'tile')
Inputs may be any that keep to these rules, and one draw needn't show every extreme that they name: Every window lies inside the object: on tile 0 the first component is 128 or more, on the last tile it is 0 or less; elsewhere it is at most 128, and the second component at most 1792. Slots at or beyond counts[t, b] also hold valid positions. Slots j < counts[t, b] of tile t and micro-batch b are live.
All inputs are finite; a program needn't handle non-finite values.
Results may differ from a plain program's by a relative error of at most 0.013.
Values may be sent and summed in bfloat16 or wider, within the bound.
No kernel may reach another device: no remote copies, remote signals or barrier semaphores. Data moves between devices by JAX's collectives and lax.ppermute only.
A program may use at most 192 MiB of HBM per device.

v0:
```python
import math

import jax
import jax.numpy as jnp
from jax import lax
from jax.sharding import PartitionSpec as P

P_SIZE = 256
M = 128
CAP = 5


def extended_2(block, sides, width):
    for axis, dim in sides:
        count = lax.axis_size(axis)
        forward = [(i, i + 1) for i in range(count - 1)]
        backward = [(target, source) for source, target in forward]
        low = lax.ppermute(
            lax.slice_in_dim(block, block.shape[dim] - width, None, axis=dim), axis, forward
        )
        high = lax.ppermute(lax.slice_in_dim(block, 0, width, axis=dim), axis, backward)
        block = jnp.concatenate([low, block, high], axis=dim)
    return block


def in_blocks(x, dim, peers):
    before, after = (x.shape[:dim], x.shape[dim + 1 :])
    return jnp.moveaxis(x.reshape(*before, peers, -1, *after), dim, 0)


def sum_at_owner(x, axis, dim):
    peers = lax.axis_size(axis)
    parts = lax.all_to_all(in_blocks(x, dim, peers), axis, 0, 0, tiled=True)
    return jnp.sum(parts, axis=0)


def shifted(value, axis, steps):
    count = lax.axis_size(axis)
    initial, last = (max(0, -steps), min(count, count - steps))
    return lax.ppermute(value, axis, [(source, source + steps) for source in range(initial, last)])


def dft_table(side_cells):
    index_of_row = jnp.arange(side_cells, dtype=jnp.int32)
    phases = index_of_row[:, None] * index_of_row[None, :] % side_cells
    angles = phases.astype(jnp.float32) * (2.0 * math.pi / side_cells)
    factor = 1.0 / math.sqrt(side_cells)
    return jnp.stack([jnp.cos(angles) * factor, -jnp.sin(angles) * factor], axis=1).astype(
        jnp.bfloat16
    )


def conj_transpose(matrix):
    flipped = jnp.transpose(matrix, (2, 1, 0))
    return jnp.stack([flipped[:, 0], -flipped[:, 1]], axis=1)


def block_pair(matrix):
    real_part = matrix[:, 0]
    imag_part = matrix[:, 1]
    side_cells = real_part.shape[0]
    upper_half = jnp.stack([real_part, -imag_part], axis=2)
    lower_half = jnp.stack([imag_part, real_part], axis=2)
    leftward_block = jnp.stack([upper_half, lower_half], axis=1)
    right_block = jnp.transpose(leftward_block, (3, 2, 1, 0)).reshape(
        2 * side_cells, 2 * side_cells
    )
    return (leftward_block.reshape(2 * side_cells, 2 * side_cells), right_block)


def transform(blocks, wave_in):
    leftward_block, right_block = blocks
    slot_count, side_cells = (wave_in.shape[0], wave_in.shape[1])
    stacked_arrays = wave_in.reshape(slot_count, 2 * side_cells, side_cells)
    central_part = jnp.einsum(
        "rj,tjg->trg", leftward_block, stacked_arrays, preferred_element_type=jnp.float32
    )
    central_part = central_part.astype(jnp.bfloat16).reshape(slot_count, side_cells, 2 * side_cells)
    result = jnp.einsum(
        "cib,bk->cik", central_part, right_block, preferred_element_type=jnp.float32
    )
    return result.reshape(slot_count, side_cells, 2, side_cells)


def complex_product(first_wave, second_wave, conjugate):
    first_real = first_wave[..., 0, :].astype(jnp.float32)
    first_imag = first_wave[..., 1, :].astype(jnp.float32)
    second_real = second_wave[..., 0, :].astype(jnp.float32)
    second_imag = second_wave[..., 1, :].astype(jnp.float32)
    if conjugate:
        first_imag = -first_imag
    return jnp.stack(
        [
            first_real * second_real - first_imag * second_imag,
            first_real * second_imag + first_imag * second_real,
        ],
        axis=-2,
    )


def cut_windows(extended, placements):

    def single(placement):
        anchor = jnp.zeros((), jnp.int32)
        return lax.dynamic_slice(
            extended,
            (anchor, placement[0], anchor, placement[1]),
            (extended.shape[0], P_SIZE, 2, P_SIZE),
        )

    return jax.vmap(single)(placements)


def add_patches(totals, patches, placements):
    for slot_no in range(patches.shape[0]):
        anchor = jnp.zeros((), jnp.int32)
        corner = (anchor, placements[slot_no, 0], anchor, placements[slot_no, 1])
        current = lax.dynamic_slice(totals, corner, patches.shape[1:])
        totals = lax.dynamic_update_slice(totals, current + patches[slot_no], corner)
    return totals


def forward_section(windows, wave_in, forward_list):
    entering = []
    leaving = None
    for slice_no in range(len(forward_list)):
        entering.append(wave_in)
        product = complex_product(windows[:, slice_no], wave_in, False).astype(jnp.bfloat16)
        leaving = transform(forward_list[slice_no], product)
        wave_in = leaving.astype(jnp.bfloat16)
    return (jnp.stack(entering, axis=0), leaving)


def backward_section(windows, entering, incoming, backward_list):
    patches = []
    for slice_no in reversed(range(len(backward_list))):
        spread = transform(backward_list[slice_no], incoming.astype(jnp.bfloat16)).astype(
            jnp.bfloat16
        )
        patches.insert(0, complex_product(entering[slice_no], spread, True))
        incoming = complex_product(windows[:, slice_no], spread, True)
    return (jnp.stack(patches, axis=1), incoming)


def far_gradient(far_field, observed, live_slots):
    real_part = far_field[:, :, 0, :]
    imag_part = far_field[:, :, 1, :]
    weight = live_slots.astype(jnp.float32)[:, None, None]
    misfit = weight * (real_part * real_part + imag_part * imag_part - observed)
    return jnp.stack([misfit * real_part, misfit * imag_part], axis=2)


def local(object_layer_slices, probe_wave, propagator, positions, counts, measured):
    section = lax.axis_index("depth")
    tile_rows = object_layer_slices.shape[1]
    extended = extended_2(object_layer_slices, (("tile", 1),), M)
    detector = dft_table(P_SIZE)
    blocks_prop = block_pair(propagator)
    adjoint_prop = block_pair(conj_transpose(propagator))
    start_wave = jnp.broadcast_to(probe_wave, (CAP, P_SIZE, 2, P_SIZE))
    slot_index = jnp.arange(CAP, dtype=jnp.int32)
    whole_extended = lax.all_gather(extended, "depth", axis=0, tiled=True)
    all_slices = whole_extended.shape[0]
    forward_list = [blocks_prop] * (all_slices - 1) + [block_pair(detector)]
    backward_list = [adjoint_prop] * (all_slices - 1) + [block_pair(conj_transpose(detector))]
    totals = jnp.zeros(whole_extended.shape, jnp.float32)
    batch_no = 0 + section
    placements = lax.dynamic_index_in_dim(positions[0], batch_no, 0, False)
    live_slots = slot_index < lax.dynamic_index_in_dim(counts[0], batch_no, 0, False)
    observed = lax.dynamic_index_in_dim(measured[0], batch_no, 0, False)
    windows = cut_windows(whole_extended, placements)
    entering, far_field = forward_section(windows, start_wave, forward_list)
    incoming = far_gradient(far_field, observed, live_slots)
    patches, incoming = backward_section(windows, entering, incoming, backward_list)
    totals = add_patches(totals, patches, placements)
    totals = sum_at_owner(totals, "depth", 0)
    lower_rim = totals[:, :M]
    upper_border = totals[:, M + tile_rows :]
    interior = totals[:, M : M + tile_rows]
    from_above = shifted(lower_rim, "tile", -1)
    from_below = shifted(upper_border, "tile", 1)
    interior = interior + from_below
    interior = interior + from_above
    return interior


def solution(mesh):
    placed = (
        P("depth", "tile", None, None),
        P(),
        P(),
        P("tile", None, None, None),
        P("tile", None),
        P("tile", None, None, None, None),
    )
    return jax.shard_map(
        local, mesh=mesh, in_specs=placed, out_specs=P("depth", "tile", None, None), check_vma=False
    )
```

profile of v0, /device:TPU:128, one launch (start us, length us, event | category | flops | bytes accessed | tf_op | source)
XLA Modules:
  0.0 669.5 jit_solution(15511454064403059577)
XLA Ops:
  6.5 2.8 copy.56
  9.4 3.4 collective-permute-start
  12.8 7.9 %collective-permute-start.1 = (f32[1,128,2,2048]{3,1,2,0:T(8,128)S(1)}, f32[1,128,2,2048]{3,1,2,0:T(8,128)S(1)}, u32[]{:S(2)}, u32[]{:S(2)}) collective-permute-start(f32[1,128,2,2048]{3,1,2,0:T(8,128)S(1)} %copy.56), channel_id=1, source_target_pairs={{1,0},{2,1},{3,2},{4,3},{5,4},{6,5},{7,6},{8,7},{9,8},{10,9},{11,1... | collective-permute-start | bytes 6291464 | tf_op jit(solution)/shard_map/ppermute | solution.py:21
  20.6 43.4 %collective-permute-done = f32[1,128,2,2048]{3,1,2,0:T(8,128)S(1)} collective-permute-done((f32[1,128,2,2048]{3,1,2,0:T(8,128)S(1)}, f32[1,128,2,2048]{3,1,2,0:T(8,128)S(1)}, u32[]{:S(2)}, u32[]{:S(2)}) %collective-permute-start) | collective-permute-done | bytes 2097184 | tf_op jit(solution)/shard_map/ppermute | solution.py:18
  64.1 1.2 collective-permute-done.1
  65.2 3.0 pad_maximum_fusion
  81.9 22.4 %copy.66 = bf16[256,2,256,2]{3,2,1,0:T(8,128)(2,1)} copy(bf16[256,2,256,2]{2,0,3,1:T(8,128)(2,1)S(1)} %get-tuple-element.53) | data formatting | bytes 1048576 | tf_op jit(solution)/shard_map/stack | solution.py:64
  104.2 49.6 %reshape.275 = bf16[512,512,1]{1,0,2:T(8,128)(2,1)} reshape(bf16[256,2,256,2]{3,2,1,0:T(8,128)(2,1)} %copy.66) | data formatting | bytes 1048576 | tf_op jit(solution)/shard_map/reshape | solution.py:68
  157.6 22.2 %copy.72 = bf16[256,2,256,2]{3,2,1,0:T(8,128)(2,1)} copy(bf16[256,2,256,2]{2,0,3,1:T(8,128)(2,1)S(1)} %get-tuple-element.51) | data formatting | bytes 1048576 | tf_op jit(solution)/shard_map/stack | solution.py:64
  179.8 49.6 %reshape.278 = bf16[512,512,1]{1,0,2:T(8,128)(2,1)} reshape(bf16[256,2,256,2]{3,2,1,0:T(8,128)(2,1)} %copy.72) | data formatting | bytes 1048576 | tf_op jit(solution)/shard_map/reshape | solution.py:68
  232.4 24.2 %copy.78 = bf16[256,2,256,2]{3,2,1,0:T(8,128)(2,1)} copy(bf16[256,2,256,2]{0,2,3,1:T(8,128)(2,1)S(1)} %get-tuple-element.49) | data formatting | bytes 1048576 | tf_op jit(solution)/shard_map/stack | solution.py:64
  256.6 49.6 %reshape.281 = bf16[512,512,1]{1,0,2:T(8,128)(2,1)} reshape(bf16[256,2,256,2]{3,2,1,0:T(8,128)(2,1)} %copy.78) | data formatting | bytes 1048576 | tf_op jit(solution)/shard_map/reshape | solution.py:68
  307.9 22.2 %copy.85 = bf16[256,2,256,2]{3,2,1,0:T(8,128)(2,1)} copy(bf16[256,2,256,2]{2,0,3,1:T(8,128)(2,1)S(1)} %get-tuple-element.47) | data formatting | bytes 1048576 | tf_op jit(solution)/shard_map/stack | solution.py:64
  330.1 49.6 %reshape.284 = bf16[512,512,1]{1,0,2:T(8,128)(2,1)} reshape(bf16[256,2,256,2]{3,2,1,0:T(8,128)(2,1)} %copy.85) | data formatting | bytes 1048576 | tf_op jit(solution)/shard_map/reshape | solution.py:68
  390.1 27.7 %while.1 = (s32[]{:T(128)}, f32[2,384,2,2048]{3,1,2,0:T(8,128)}, s32[5,4]{0,1:T(4,128)S(1)}, f32[5,2,256,2,256]{4,2,3,0,1:T(8,128)}, s32[]{:T(128)}) while((s32[]{:T(128)}, f32[2,384,2,2048]{3,1,2,0:T(8,128)}, s32[5,4]{0,1:T(4,128)S(1)}, f32[5,2,256,2,256]{4,2,3,0,1:T(8,128)}, s32[]{:T(128)}) %tuple.56), condition=%wide.while_cond, body=%wide.while_body.sunk | while | flops 2 | bytes 6292089 | solution.py:105
  390.7 3.0 constant_dynamic-slice_fusion.7
  396.3 3.0 constant_dynamic-slice_fusion.7
  401.8 3.0 constant_dynamic-slice_fusion.7
  405.6 1.1 copy_dynamic-update-slice_fusion.2
  407.4 3.0 constant_dynamic-slice_fusion.7
  412.9 3.0 constant_dynamic-slice_fusion.7
  417.8 3.0 slice_bitcast_fusion
  421.3 2.4 copy.63
  423.7 4.1 convert_element_type.184
  427.8 3.4 fusion.1
  431.2 2.5 copy.68
  433.7 3.2 reshape.276
  436.8 2.3 convolution_convert_fusion.5
  440.4 2.4 copy.71
  442.8 4.5 convert_element_type.190
  447.3 3.4 fusion.2
  450.7 2.4 copy.74
  453.1 3.2 reshape.279
  456.3 2.3 fusion.20
  459.6 2.4 copy.77
  462.0 4.2 convert_element_type.194
  466.1 3.3 fusion.3
  469.4 2.4 copy.80
  471.8 3.2 reshape.282
  475.1 2.3 convolution_convert_fusion.2
  477.4 2.4 fusion.15
  479.9 1.4 copy.83
  482.3 2.0 fusion.4
  484.3 1.6 copy.87
  485.9 1.5 reshape.285
  487.4 2.1 maximum_bitcast_fusion.1
  491.1 1.5 copy-done.2
  493.6 6.1 broadcast_in_dim.4
  499.7 11.7 %dynamic_update_slice.16 = f32[2,384,2,2048]{3,1,2,0:T(8,128)} dynamic-update-slice(f32[2,384,2,2048]{3,1,2,0:T(8,128)} %broadcast_in_dim.4, f32[2,256,2,256]{3,1,2,0:T(8,128)} %fusion.27, s32[]{:T(128)} %constant.28.clone.1, s32[]{:T(128)S(6)} %select_n.86, s32[]{:T(128)} %constant.28.clone.1, s32[]{:T(128)S(6)} %select_n.87) | dynamic-update-slice | bytes 2097156 | tf_op jit(solution)/shard_map/dynamic_update_slice | solution.py:119
  511.4 2.9 fusion.30
  514.4 11.7 %dynamic_update_slice.17 = f32[2,384,2,2048]{3,1,2,0:T(8,128)} dynamic-update-slice(f32[2,384,2,2048]{3,1,2,0:T(8,128)} %dynamic_update_slice.16, f32[2,256,2,256]{3,1,2,0:T(8,128)} %fusion.30, s32[]{:T(128)} %constant.28.clone.1, s32[]{:T(128)S(6)} %select_n.88, s32[]{:T(128)} %constant.28.clone.1, s32[]{:T(128)S(6)} %select_n.89) | dynamic-update-slice | bytes 2097156 | tf_op jit(solution)/shard_map/dynamic_update_slice | solution.py:119
  526.1 2.9 fusion.33
  529.0 11.9 %dynamic_update_slice.18 = f32[2,384,2,2048]{3,1,2,0:T(8,128)} dynamic-update-slice(f32[2,384,2,2048]{3,1,2,0:T(8,128)} %dynamic_update_slice.17, f32[2,256,2,256]{3,1,2,0:T(8,128)} %fusion.33, s32[]{:T(128)} %constant.28.clone.1, s32[]{:T(128)S(6)} %select_n.90, s32[]{:T(128)} %constant.28.clone.1, s32[]{:T(128)S(6)} %select_n.91) | dynamic-update-slice | bytes 2097156 | tf_op jit(solution)/shard_map/dynamic_update_slice | solution.py:119
  540.9 2.9 fusion.25
  543.8 11.2 %dynamic_update_slice.19 = f32[2,384,2,2048]{3,1,2,0:T(8,128)} dynamic-update-slice(f32[2,384,2,2048]{3,1,2,0:T(8,128)} %dynamic_update_slice.18, f32[2,256,2,256]{3,1,2,0:T(8,128)} %fusion.25, s32[]{:T(128)} %constant.28.clone.1, s32[]{:T(128)S(6)} %select_n.92, s32[]{:T(128)} %constant.28.clone.1, s32[]{:T(128)S(6)} %select_n.93) | dynamic-update-slice | bytes 2097156 | tf_op jit(solution)/shard_map/dynamic_update_slice | solution.py:119
  555.0 2.9 fusion.36
  558.0 11.6 %dynamic_update_slice.20 = f32[2,1,384,2,2048]{4,2,3,0,1:T(8,128)} dynamic-update-slice(f32[2,1,384,2,2048]{4,2,3,0,1:T(8,128)} %bitcast.208, f32[2,1,256,2,256]{4,2,3,0,1:T(8,128)} %fusion.36, s32[]{:T(128)} %constant.28.clone.1, s32[]{:T(128)} %constant.28.clone.1, s32[]{:T(128)S(6)} %select_n.94, s32[]{:T(128)} %constant.28.clone.1, s32[]{:T(128)S(6)} %select_n.95) | dynamic-update-slice | bytes 2097156 | tf_op jit(solution)/shard_map/dynamic_update_slice | solution.py:119
  569.6 25.0 %all_to_all.5 = f32[2,1,384,2,2048]{4,2,3,1,0:T(8,128)} all-to-all(f32[2,1,384,2,2048]{4,2,3,1,0:T(8,128)} %bitcast.209), channel_id=1, replica_groups=mesh['depth'=2,'tile'=128] {'depth'}, dimensions={0} | all-to-all | bytes 25165824 | tf_op jit(solution)/shard_map/all_to_all | solution.py:33
  594.6 6.9 %bitcast_reduce_fusion = f32[384,2,2048]{2,0,1:T(8,128)S(1)} fusion(f32[2,1,384,2,2048]{4,2,3,1,0:T(8,128)} %all_to_all.5), kind=kLoop, calls=%fused_computation.4 | loop fusion | flops 1572864 | bytes 18874368 | tf_op jit(solution)/shard_map/reduce_sum | solution.py:34
  601.8 1.9 collective-permute-start.2
  603.7 10.1 %collective-permute-start.3 = (f32[1,128,2,2048]{3,1,2,0:T(8,128)S(1)}, f32[1,128,2,2048]{3,1,2,0:T(8,128)S(1)}, u32[]{:S(2)}, u32[]{:S(2)}) collective-permute-start(f32[1,128,2,2048]{3,1,2,0:T(8,128)S(1)} %get-tuple-element.30), channel_id=1, source_target_pairs={{1,0},{2,1},{3,2},{4,3},{5,4},{6,5},{7,6},{8,7},{9,8},{10,9},{11,1... | collective-permute-start | bytes 6291464 | tf_op jit(solution)/shard_map/ppermute | solution.py:40
  613.9 44.0 %collective-permute-done.2 = f32[1,128,2,2048]{3,1,2,0:T(8,128)S(1)} collective-permute-done((f32[1,128,2,2048]{3,1,2,0:T(8,128)S(1)}, f32[1,128,2,2048]{3,1,2,0:T(8,128)S(1)}, u32[]{:S(2)}, u32[]{:S(2)}) %collective-permute-start.2) | collective-permute-done | bytes 2097184 | tf_op jit(solution)/shard_map/ppermute | solution.py:40
  657.8 1.2 collective-permute-done.3
  659.5 2.9 copy.96
  (110 shorter events, 33.0 us)
Async XLA Ops:
  6.5 61.7 %copy-start = (s32[1,2,5,2]{2,3,1,0:T(2,128)S(1)}, s32[1,2,5,2]{2,3,1,0:T(2,128)}, u32[]{:S(2)}) copy-start(s32[1,2,5,2]{2,3,1,0:T(2,128)} %param.9) | copy-start | bytes 244
  6.5 383.6 %all-gather.2.cloned.1.call-start = ((), (), s32[]{:S(2)}) async-start(), calls=%async_computation.1 | async-start | bytes 18874368 | tf_op jit(solution)/shard_map/all_gather | solution.py:162
  9.4 54.7 %collective-permute-start = (f32[1,128,2,2048]{3,1,2,0:T(8,128)S(1)}, f32[1,128,2,2048]{3,1,2,0:T(8,128)S(1)}, u32[]{:S(2)}, u32[]{:S(2)}) collective-permute-start(f32[1,128,2,2048]{3,1,2,0:T(8,128)S(1)} %copy.56), channel_id=1, source_target_pairs={{0,1},{1,2},{2,3},{3,4},{4,5},{5,6},{6,7},{7,8},{8,9},{9,10},{10,1... | collective-permute-start | bytes 6291464 | tf_op jit(solution)/shard_map/ppermute | solution.py:18
  12.8 52.5 %collective-permute-start.1 = (f32[1,128,2,2048]{3,1,2,0:T(8,128)S(1)}, f32[1,128,2,2048]{3,1,2,0:T(8,128)S(1)}, u32[]{:S(2)}, u32[]{:S(2)}) collective-permute-start(f32[1,128,2,2048]{3,1,2,0:T(8,128)S(1)} %copy.56), channel_id=1, source_target_pairs={{1,0},{2,1},{3,2},{4,3},{5,4},{6,5},{7,6},{8,7},{9,8},{10,9},{11,1... | collective-permute-start | bytes 6291464 | tf_op jit(solution)/shard_map/ppermute | solution.py:21
  68.2 12.9 %copy-start.5 = (bf16[256,2,256]{2,1,0:T(2,128)(2,1)S(1)}, bf16[256,2,256]{2,1,0:T(2,128)(2,1)}, u32[]{:S(2)}) copy-start(bf16[256,2,256]{2,1,0:T(2,128)(2,1)} %param.8) | copy-start | bytes 786436
  229.8 0.7 copy-start.15
  380.3 7.9 %copy-start.8 = (bf16[256,2,256]{2,1,0:T(2,128)(2,1)S(1)}, bf16[256,2,256]{2,1,0:T(2,128)(2,1)}, u32[]{:S(2)}) copy-start(bf16[256,2,256]{2,1,0:T(2,128)(2,1)} %param.7) | copy-start | bytes 786436
  417.8 3.0 copy-start.9
  439.1 1.1 copy-start.3
  456.3 2.4 copy-start.10
  462.0 4.2 copy-start.11
  471.8 3.2 copy-start.13
  475.1 2.3 copy-start.4
  481.3 1.0 copy-start.12
  487.3 2.2 copy-start.6
  487.3 2.2 copy-start.14
  489.6 0.9 copy-start.7
  491.1 1.5 copy-start.2
  601.8 56.1 %collective-permute-start.2 = (f32[1,128,2,2048]{3,1,2,0:T(8,128)S(1)}, f32[1,128,2,2048]{3,1,2,0:T(8,128)S(1)}, u32[]{:S(2)}, u32[]{:S(2)}) collective-permute-start(f32[1,128,2,2048]{3,1,2,0:T(8,128)S(1)} %get-tuple-element.29), channel_id=1, source_target_pairs={{0,1},{1,2},{2,3},{3,4},{4,5},{5,6},{6,7},{7,8},{8,9},{9,10},{10,1... | collective-permute-start | bytes 6291464 | tf_op jit(solution)/shard_map/ppermute | solution.py:40
  603.7 55.3 %collective-permute-start.3 = (f32[1,128,2,2048]{3,1,2,0:T(8,128)S(1)}, f32[1,128,2,2048]{3,1,2,0:T(8,128)S(1)}, u32[]{:S(2)}, u32[]{:S(2)}) collective-permute-start(f32[1,128,2,2048]{3,1,2,0:T(8,128)S(1)} %get-tuple-element.30), channel_id=1, source_target_pairs={{1,0},{2,1},{3,2},{4,3},{5,4},{6,5},{7,6},{8,7},{9,8},{10,9},{11,1... | collective-permute-start | bytes 6291464 | tf_op jit(solution)/shard_map/ppermute | solution.py:40
  659.0 3.5 copy-start.1
Sparse Core Ops, SparseCore 0:
  68.4 31.8 all-gather.1
where the time goes:
time: 680 us; the launch traced here: 670 us
  local copies, waits for them, and re-layouts  443 us (65%)
  waiting for transfers between devices  89.8 us (13%)
  other arithmetic  36.4 us (5%)
  between operations  32.4 us (5%)
  blocking collectives  25 us (4%)
  starting transfers between devices  23.3 us (3%)
  matrix products  19.8 us (3%)
    reshape x4, local copies, waits for them, and re-layouts, block_pair(): return (leftward_block.reshape(2 * side_cells, 2 * side_cells), right_block)  198 us
    another operation x4, local copies, waits for them, and re-layouts, block_pair(): leftward_block = jnp.stack([upper_half, lower_half], axis=1)  90.9 us
    dynamic_update_slice x5, local copies, waits for them, and re-layouts, add_patches(): lax.dynamic_update_slice(totals, current + patches[slot_no], corner)  58 us
    ppermute x2, waiting for transfers between devices, shifted(): lax.ppermute(value, axis, [(source, source + steps) for source in range(i...  45.2 us
    ppermute x1, waiting for transfers between devices, extended_2(): lax.ppermute(lax.slice_in_dim(block, block.shape[dim] - width, None, axis...  43.4 us
    gather x25, local copies, waits for them, and re-layouts  27.6 us
    all_to_all x1, blocking collectives, sum_at_owner(): parts = lax.all_to_all(in_blocks(x, dim, peers), axis, 0, 0, tiled=True)  25 us
  transfers between devices with their start and end apart: 5, of which 4 were waited for; matrix products, arithmetic and copies ran while one was open for 45% of the time, Pallas kernels for 0%

commit v1 on v0

v1 whole, which is shorter than its diff:
```python
import jax
import jax.numpy as jnp
import numpy as np
from jax import lax
from jax.experimental import pallas as pl
from jax.experimental.pallas import tpu as pltpu
from jax.sharding import PartitionSpec as P

SIDE = 256
M = 128
CAP = 5
LW = 2048
LANES = 128
WIDE = SIDE + LANES
BLOCKS = LW // LANES
GROUP = 8
MIB = 1024 * 1024


def dft_planes():
    n = np.arange(SIDE)
    angles = (n[:, None] * n[None, :] % SIDE) * (2.0 * np.pi / SIDE)
    factor = 1.0 / np.sqrt(SIDE)
    return (
        (np.cos(angles) * factor).astype(jnp.bfloat16),
        (-np.sin(angles) * factor).astype(jnp.bfloat16),
    )


def real_form(xp, re, im):
    return xp.concatenate(
        [xp.concatenate([re, -im], axis=1), xp.concatenate([im, re], axis=1)], axis=0
    )


def as_lines(block):
    rows = block.shape[0]
    lines = block.reshape(rows, 2, BLOCKS, LANES).transpose(0, 2, 1, 3)
    return lines.reshape(rows * 2 * BLOCKS, LANES)


def from_lines(lines):
    rows = lines.shape[0] // (2 * BLOCKS)
    block = lines.reshape(rows, BLOCKS, 2, LANES).transpose(0, 2, 1, 3)
    return block.reshape(rows, 2, LW)


def planes_kernel(lines_ref, planes_ref):
    for block in range(BLOCKS):
        for part in range(2):
            cells = lines_ref[pl.ds(2 * block + part, M, stride=2 * BLOCKS), :]
            planes_ref[part, :, block * LANES : (block + 1) * LANES] = cells.astype(
                jnp.bfloat16
            )


def split_planes(lines):
    return pl.pallas_call(
        planes_kernel,
        out_shape=jax.ShapeDtypeStruct((2, M, LW), jnp.bfloat16),
        in_specs=[pl.BlockSpec(memory_space=pltpu.VMEM)],
        out_specs=pl.BlockSpec(memory_space=pltpu.VMEM),
        compiler_params=pltpu.CompilerParams(vmem_limit_bytes=16 * MIB),
        name="split_planes",
    )(lines)


def total_kernel(inner_ref, other_ref, above_ref, below_ref, lines_ref):
    for block in range(BLOCKS):
        cols = slice(block * LANES, (block + 1) * LANES)
        for part in range(2):
            cells = inner_ref[part, :, cols] + other_ref[part, :, cols].astype(jnp.float32)
            cells = cells + below_ref[part, :, cols].astype(jnp.float32)
            cells = cells + above_ref[part, :, cols].astype(jnp.float32)
            lines_ref[pl.ds(2 * block + part, M, stride=2 * BLOCKS), :] = cells


def add_up(inner, other, above, below):
    return pl.pallas_call(
        total_kernel,
        out_shape=jax.ShapeDtypeStruct((M * 2 * BLOCKS, LANES), jnp.float32),
        in_specs=[pl.BlockSpec(memory_space=pltpu.VMEM)] * 4,
        out_specs=pl.BlockSpec(memory_space=pltpu.VMEM),
        compiler_params=pltpu.CompilerParams(vmem_limit_bytes=32 * MIB),
        name="add_up",
    )(inner, other, above, below)


def product(a_re, a_im, b_re, b_im):
    return a_re * b_re - a_im * b_im, a_re * b_im + a_im * b_re


def conj_product(a_re, a_im, b_re, b_im):
    return a_re * b_re + a_im * b_im, a_re * b_im - a_im * b_re


def transform(left, right, wave_re, wave_im):
    stacked = jnp.concatenate([wave_re, wave_im], axis=0).astype(jnp.bfloat16)
    middle = jnp.dot(left, stacked, preferred_element_type=jnp.float32)
    middle = middle.astype(jnp.bfloat16)
    middle = jnp.concatenate([middle[:SIDE], middle[SIDE:]], axis=1)
    result = jnp.dot(middle, right, preferred_element_type=jnp.float32)
    return result[:, :SIDE], result[:, SIDE:]


def rounded(wave):
    return tuple(plane.astype(jnp.bfloat16).astype(jnp.float32) for plane in wave)


def probes_kernel(
    section_ref,
    places_ref,
    counts_ref,
    own_ref,
    own_o_ref,
    low_ref,
    low_o_ref,
    up_ref,
    up_o_ref,
    observed_ref,
    probe_ref,
    prop_ref,
    prop_t_ref,
    dft_ref,
    dft_t_ref,
    inner_out,
    inner_o_out,
    low_out,
    low_o_out,
    up_out,
    up_o_out,
    ext,
    observed,
    window,
    totals,
    rims,
    psi1,
    in_sems,
    out_sems,
):
    mine = section_ref[0]
    other = 1 - mine
    loads = [
        pltpu.make_async_copy(source, ext.at[slice_no, part], in_sems.at[k])
        for k, (source, slice_no, part) in enumerate(
            (
                (own_ref, mine, 1),
                (own_o_ref, other, 1),
                (low_ref, mine, 0),
                (low_o_ref, other, 0),
                (up_ref, mine, 2),
                (up_o_ref, other, 2),
            )
        )
    ]
    loads.append(pltpu.make_async_copy(observed_ref.at[mine], observed, in_sems.at[6]))
    for load in loads:
        load.start()
    totals[...] = jnp.zeros_like(totals)
    for load in loads:
        load.wait()

    rim_row = lax.broadcasted_iota(jnp.int32, (M, WIDE), 0)
    lane_of_rim = lax.broadcasted_iota(jnp.int32, (M, LANES), 1)
    lane = lax.broadcasted_iota(jnp.int32, (SIDE + GROUP, LANES), 1)
    line = lax.broadcasted_iota(jnp.int32, (SIDE // GROUP, GROUP, SIDE), 1)
    line_out = lax.broadcasted_iota(jnp.int32, (1, GROUP, SIDE), 1)
    probe_re = probe_ref[0].astype(jnp.float32)
    probe_im = probe_ref[1].astype(jnp.float32)

    for slot in range(CAP):
        row = places_ref[mine * CAP + slot, 0]
        col = places_ref[mine * CAP + slot, 1]
        base = pl.multiple_of(jnp.minimum(col // LANES, BLOCKS - 3) * LANES, LANES)
        offset = col - base
        back = lax.rem(LANES - offset, LANES)
        forth = lax.rem(offset, LANES)
        row_base = pl.multiple_of(jnp.minimum(row // GROUP, M // GROUP - 1) * GROUP, GROUP)
        row_offset = row - row_base
        row_back = lax.rem(GROUP - row_offset, GROUP)
        row_forth = lax.rem(row_offset, GROUP)

        def to_left(cells):
            turned = [
                pltpu.roll(cells[:, k * LANES : (k + 1) * LANES], back, 1) for k in range(3)
            ]
            keep = lane_of_rim < LANES - offset
            return [jnp.where(keep, turned[k], turned[k + 1]) for k in range(2)]

        def cut(slice_no, part):
            cols = pl.ds(base, WIDE)
            rim = jnp.where(
                rim_row >= row,
                ext[slice_no, 0, part, :, cols].astype(jnp.float32),
                ext[slice_no, 2, part, :, cols].astype(jnp.float32),
            )
            rim = to_left(rim)
            middle = to_left(ext[slice_no, 1, part, :, cols].astype(jnp.float32))
            for k in range(2):
                here = slice(k * LANES, (k + 1) * LANES)
                window[slice_no, part, 0:M, here] = rim[k]
                window[slice_no, part, M : 2 * M, here] = middle[k]
                window[slice_no, part, 2 * M : 3 * M, here] = rim[k]

        def load_plane(slice_no, part):
            cells = window[slice_no, part, pl.ds(row_base, SIDE + GROUP), :]
            cells = pltpu.roll(cells.reshape(SIDE // GROUP + 1, GROUP, SIDE), row_back, 1)
            cells = jnp.where(line < GROUP - row_offset, cells[:-1], cells[1:])
            return cells.reshape(SIDE, SIDE)

        def load_window(slice_no):
            return load_plane(slice_no, 0), load_plane(slice_no, 1)

        def add_patch(slice_no, patch):
            for part in range(2):
                cells = pltpu.roll(patch[part].reshape(SIDE // GROUP, GROUP, SIDE), row_forth, 1)
                late = line_out >= row_offset
                cells = jnp.concatenate(
                    [
                        jnp.where(late, cells[:1], 0.0),
                        jnp.where(line[1:] >= row_offset, cells[1:], cells[:-1]),
                        jnp.where(late, 0.0, cells[-1:]),
                    ],
                    axis=0,
                ).reshape(SIDE + GROUP, SIDE)
                turned = [
                    pltpu.roll(cells[:, k * LANES : (k + 1) * LANES], forth, 1) for k in range(2)
                ]
                late = lane >= offset
                spread = jnp.concatenate(
                    [
                        jnp.where(late, turned[0], 0.0),
                        jnp.where(late, turned[1], turned[0]),
                        jnp.where(late, 0.0, turned[1]),
                    ],
                    axis=1,
                )
                totals[slice_no, part, pl.ds(row_base, SIDE + GROUP), pl.ds(base, WIDE)] += spread

        for slice_no in range(2):
            for part in range(2):
                cut(slice_no, part)

        phi = product(probe_re, probe_im, *load_window(0))
        wave = transform(prop_ref[...], prop_t_ref[...], *phi)
        psi1[0] = wave[0].astype(jnp.bfloat16)
        psi1[1] = wave[1].astype(jnp.bfloat16)
        phi = product(*rounded(wave), *load_window(1))
        far_re, far_im = transform(dft_ref[...], dft_t_ref[...], *phi)
        live = (slot < counts_ref[mine]).astype(jnp.float32)
        misfit = live * (far_re * far_re + far_im * far_im - observed[slot])
        spread = rounded(
            transform(dft_t_ref[...], dft_ref[...], misfit * far_re, misfit * far_im)
        )
        entering = (psi1[0].astype(jnp.float32), psi1[1].astype(jnp.float32))
        add_patch(1, conj_product(*entering, *spread))
        incoming = conj_product(*load_window(1), *spread)
        spread = rounded(transform(prop_t_ref[...], prop_ref[...], *incoming))
        add_patch(0, conj_product(probe_re, probe_im, *spread))

    stores = []

    def send(k, slice_no, first_row, target):
        rims[k] = totals[slice_no, :, first_row : first_row + M, :].astype(jnp.bfloat16)
        store = pltpu.make_async_copy(rims.at[k], target, out_sems.at[k])
        store.start()
        stores.append(store)

    send(0, other, 0, low_o_out)
    send(1, other, 2 * M, up_o_out)
    send(2, mine, 0, low_out)
    send(3, mine, 2 * M, up_out)
    send(4, other, M, inner_o_out)
    store = pltpu.make_async_copy(
        totals.at[mine, :, pl.ds(M, M), :], inner_out, out_sems.at[5]
    )
    store.start()
    stores.append(store)
    for store in stores:
        store.wait()


def probes(section, places, counts, planes, observed, probe, matrices):
    smem = pl.BlockSpec(memory_space=pltpu.SMEM)
    vmem = pl.BlockSpec(memory_space=pltpu.VMEM)
    apart = pl.BlockSpec(memory_space=pl.ANY)
    rim = jax.ShapeDtypeStruct((2, M, LW), jnp.bfloat16)
    return pl.pallas_call(
        probes_kernel,
        out_shape=[jax.ShapeDtypeStruct((2, M, LW), jnp.float32)] + [rim] * 5,
        in_specs=[smem] * 3 + [apart] * 7 + [vmem] * 5,
        out_specs=[apart] * 6,
        scratch_shapes=[
            pltpu.VMEM((2, 3, 2, M, LW), jnp.bfloat16),
            pltpu.VMEM((CAP, SIDE, SIDE), jnp.float32),
            pltpu.VMEM((2, 2, 3 * M, SIDE), jnp.float32),
            pltpu.VMEM((2, 2, 3 * M, LW), jnp.float32),
            pltpu.VMEM((5, 2, M, LW), jnp.bfloat16),
            pltpu.VMEM((2, SIDE, SIDE), jnp.bfloat16),
            pltpu.SemaphoreType.DMA((7,)),
            pltpu.SemaphoreType.DMA((6,)),
        ],
        compiler_params=pltpu.CompilerParams(vmem_limit_bytes=56 * MIB),
        name="probes",
    )(section, places, counts, *planes, observed, probe, *matrices)


def moved(value, steps):
    count = lax.axis_size("tile")
    first, last = (max(0, -steps), min(count, count - steps))
    return lax.ppermute(value, "tile", [(source, source + steps) for source in range(first, last)])


def across(value):
    return lax.ppermute(value, "depth", [(0, 1), (1, 0)])


def local(object_layer_slices, probe_wave, propagator, positions, counts, measured):
    own = split_planes(as_lines(object_layer_slices[0]))
    low = moved(own, 1)
    up = moved(own, -1)
    own_o = across(own)
    low_o = across(low)
    up_o = across(up)

    section = lax.axis_index("depth").astype(jnp.int32).reshape(1)
    probe = jnp.stack([probe_wave[:, 0], probe_wave[:, 1]])
    prop = real_form(jnp, propagator[:, 0], propagator[:, 1])
    dft = real_form(np, *dft_planes())
    matrices = (prop, prop.T, jnp.asarray(dft), jnp.asarray(dft.T.copy()))
    inner, inner_o, low_g, low_og, up_g, up_og = probes(
        section,
        positions.reshape(2 * CAP, 2),
        counts.reshape(2),
        (own, own_o, low, low_o, up, up_o),
        measured[0],
        probe,
        matrices,
    )
    above = moved(low_g + across(low_og), -1)
    below = moved(up_g + across(up_og), 1)
    lines = add_up(inner, across(inner_o), above, below)
    return from_lines(lines)[None]


def solution(mesh):
    placed = (
        P("depth", "tile", None, None),
        P(),
        P(),
        P("tile", None, None, None),
        P("tile", None),
        P("tile", None, None, None, None),
    )
    return jax.shard_map(
        local, mesh=mesh, in_specs=placed, out_specs=P("depth", "tile", None, None), check_vma=False
    )
```

time: 680 us -> 113 us (0.17); the launches traced: 670 us -> 112 us
  local copies, waits for them, and re-layouts: 443 us -> 4.49 us
  other arithmetic: 36.4 us -> 3.64 us
  between operations: 32.4 us -> 0.19 us
  waiting for transfers between devices: 89.8 us -> 60.8 us
  Pallas kernels: 0 us -> 27.3 us
  blocking collectives: 25 us -> 0 us
  matrix products: 19.8 us -> 0 us
  starting transfers between devices: 23.3 us -> 15.9 us
    reshape x8 -> x2, local copies, waits for them, and re-layouts: 209 us -> 0.76 us  [local(): positions.reshape(2 * CAP, 2)]
    another operation x11 -> x1, local copies, waits for them, and re-layouts: 99.5 us -> 0.04 us  [local(): probe = jnp.stack([probe_wave[:, 0], probe_wave[:, 1]])]
    dynamic_update_slice x5 -> x0, local copies, waits for them, and re-layouts: 58 us -> none  [add_patches(): lax.dynamic_update_slice(totals, current + patches[slot_no], corner)]
    ppermute x4 -> x10, waiting for transfers between devices: 89.8 us -> 60.8 us  [the longest x4 58.8 us: moved(): lax.ppermute(value, 'tile', [(source, source + steps) for source in range...]
    gather x25 -> x0, local copies, waits for them, and re-layouts: 27.6 us -> none
    pallas_call x0 -> x3, Pallas kernels: none -> 27.3 us  [the longest x1 22 us: probes(): pl.pallas_call(probes_kernel, out_shape=[jax.ShapeDtypeStruct((2, M, LW),...]
    all_to_all x1 -> x0, blocking collectives: 25 us -> none  [sum_at_owner(): parts = lax.all_to_all(in_blocks(x, dim, peers), axis, 0, 0, tiled=True)]
    convert_element_type x8 -> x0, local copies, waits for them, and re-layouts: 22.2 us -> none  [the longest x4 8.93 us: transform(): central_part.astype(jnp.bfloat16)]
  transfers between devices with their start and end apart: 5 -> 10, of which waited for: 4 -> 5; matrix products, arithmetic and copies ran while one was open for 45% -> 6% of each run, Pallas kernels for 0% -> 0%
where the time goes in v1:
time: 113 us; the launch traced here: 112 us
  waiting for transfers between devices  60.8 us (54%)
  Pallas kernels  27.3 us (24%)
  starting transfers between devices  15.9 us (14%)
  local copies, waits for them, and re-layouts  4.49 us (4%)
  other arithmetic  3.64 us (3%)
    ppermute x4, waiting for transfers between devices, moved(): lax.ppermute(value, 'tile', [(source, source + steps) for source in range...  58.8 us
    pallas_call x1, Pallas kernels, probes(): pl.pallas_call(probes_kernel, out_shape=[jax.ShapeDtypeStruct((2, M, LW),...  22 us
    ppermute x4, starting transfers between devices, moved(): lax.ppermute(value, 'tile', [(source, source + steps) for source in range...  14.7 us
    pallas_call x1, Pallas kernels, add_up(): pl.pallas_call(total_kernel, out_shape=jax.ShapeDtypeStruct((M * 2 * BLOC...  3.67 us
  transfers between devices with their start and end apart: 10, of which 5 were waited for; matrix products, arithmetic and copies ran while one was open for 6% of the time, Pallas kernels for 0%

profile of v1, /device:TPU:128, one launch (start us, length us, event | category | flops | bytes accessed | tf_op | source)
XLA Modules:
  0.0 112.3 jit_solution(8866455131568756126)
XLA Ops:
  0.0 0.0 copy-start.2
  0.0 1.6 %copy-done.2 = f32[1,128,2,2048]{3,2,1,0:T(2,128)S(1)} copy-done((f32[1,128,2,2048]{3,2,1,0:T(2,128)S(1)}, f32[1,128,2,2048]{3,2,1,0:T(2,128)}, u32[]{:S(2)}) %copy-start.2) | copy-done | bytes 2097176
  1.6 0.0 copy-start.5
  1.6 0.0 copy-start.7
  1.6 1.7 %split_planes.1.own_ref = bf16[2,128,2048]{2,1,0:T(8,128)(2,1)S(1)} custom-call(f32[4096,128]{1,0:T(8,128)S(1)} %bitcast.24), custom_call_target="tpu_custom_call" | custom-call | tf_op jit(solution)/shard_map/split_planes/pallas_call | solution.py:58
  3.3 0.0 copy-start
  3.3 0.0 copy-start.6
  3.3 6.8 %collective-permute-start.3 = (bf16[2,128,2048]{2,1,0:T(8,128)(2,1)S(1)}, bf16[2,128,2048]{2,1,0:T(8,128)(2,1)S(1)}, u32[]{:S(2)}, u32[]{:S(2)}) collective-permute-start(bf16[2,128,2048]{2,1,0:T(8,128)(2,1)S(1)} %split_planes.1.own_ref), channel_id=1, source_target_pairs={{1,0},{2,1},{3,2},{4,3},{5,4},{6,5},{7,6},{8,7},{9,8},{10,9},{11,1... | collective-permute-start | bytes 3145736 | tf_op jit(solution)/shard_map/ppermute | solution.py:311
  10.1 1.9 %collective-permute-start.1 = (bf16[2,128,2048]{2,1,0:T(8,128)(2,1)S(1)}, bf16[2,128,2048]{2,1,0:T(8,128)(2,1)}, u32[]{:S(2)}, u32[]{:S(2)}) collective-permute-start(bf16[2,128,2048]{2,1,0:T(8,128)(2,1)S(1)} %split_planes.1.own_ref), channel_id=1, source_target_pairs={{0,1},{1,2},{2,3},{3,4},{4,5},{5,6},{6,7},{7,8},{8,9},{9,10},{10,1... | collective-permute-start | bytes 3145736 | tf_op jit(solution)/shard_map/ppermute | solution.py:311
  12.0 0.1 collective-permute-start
  12.1 20.4 %collective-permute-done.3.up_ref = bf16[2,128,2048]{2,1,0:T(8,128)(2,1)S(1)} collective-permute-done((bf16[2,128,2048]{2,1,0:T(8,128)(2,1)S(1)}, bf16[2,128,2048]{2,1,0:T(8,128)(2,1)S(1)}, u32[]{:S(2)}, u32[]{:S(2)}) %collective-permute-start.3) | collective-permute-done | bytes 1048608 | tf_op jit(solution)/shard_map/ppermute | solution.py:311
  32.5 0.0 copy-start.3
  32.5 0.0 collective-permute-start.4
  32.5 9.6 %collective-permute-done.1.low_ref = bf16[2,128,2048]{2,1,0:T(8,128)(2,1)} collective-permute-done((bf16[2,128,2048]{2,1,0:T(8,128)(2,1)S(1)}, bf16[2,128,2048]{2,1,0:T(8,128)(2,1)}, u32[]{:S(2)}, u32[]{:S(2)}) %collective-permute-start.1) | collective-permute-done | bytes 1048608 | tf_op jit(solution)/shard_map/ppermute | solution.py:311
  42.1 0.0 collective-permute-start.2
  42.1 0.0 copy-done.5
  42.1 0.4 fusion.1
  42.5 0.0 copy-done.7
  42.5 0.1 reshape.16
  42.6 0.7 copy.15.places_ref
  43.3 0.1 copy.21
  43.5 0.1 copy.20
  43.6 0.9 fusion
  44.5 1.0 copy.16.prop_ref
  45.5 0.0 copy-done
  45.5 0.0 copy-done.3
  45.5 0.0 copy-done.6
  45.5 0.4 fusion.2
  46.0 0.8 pad_maximum_fusion.probe_ref
  46.7 0.0 collective-permute-done.own_o_ref
  46.7 0.0 collective-permute-done.4.up_o_ref
  46.7 0.0 collective-permute-done.2.low_o_ref
  46.7 22.0 %probes.1 = (f32[2,128,2048]{2,1,0:T(8,128)}, bf16[2,128,2048]{2,1,0:T(8,128)(2,1)}, bf16[2,128,2048]{2,1,0:T(8,128)(2,1)}, bf16[2,128,2048]{2,1,0:T(8,128)(2,1)...) custom-call(s32[1]{0:T(128)} %bitcast.section_ref, s32[10,2]{1,0:T(8,128)} %copy.15.places_ref, ...), custom_call_target="tpu_custom_call" | custom-call | tf_op jit(solution)/shard_map/probes/pallas_call | solution.py:288
  68.7 0.0 copy-start.4
  68.7 0.5 collective-permute-start.6
  69.3 0.1 collective-permute-start.8
  69.4 0.4 collective-permute-start.5
  69.8 2.0 %collective-permute-done.6 = bf16[2,128,2048]{2,1,0:T(8,128)(2,1)S(1)} collective-permute-done((bf16[2,128,2048]{2,1,0:T(8,128)(2,1)}, bf16[2,128,2048]{2,1,0:T(8,128)(2,1)S(1)}, u32[]{:S(2)}, u32[]{:S(2)}) %collective-permute-start.6) | collective-permute-done | bytes 1048608 | tf_op jit(solution)/shard_map/ppermute | solution.py:315
  71.8 1.6 %add.6 = bf16[2,128,2048]{2,1,0:T(8,128)(2,1)S(1)} add(bf16[2,128,2048]{2,1,0:T(8,128)(2,1)} %get-tuple-element.13, bf16[2,128,2048]{2,1,0:T(8,128)(2,1)S(1)} %collective-permute-done.6) | non-fusion elementwise | flops 524288 | bytes 3145728 | tf_op jit(solution)/shard_map/add | solution.py:340
  73.4 0.0 copy-start.1
  73.4 2.1 %collective-permute-start.7 = (bf16[2,128,2048]{2,1,0:T(8,128)(2,1)S(1)}, bf16[2,128,2048]{2,1,0:T(8,128)(2,1)S(1)}, u32[]{:S(2)}, u32[]{:S(2)}) collective-permute-start(bf16[2,128,2048]{2,1,0:T(8,128)(2,1)S(1)} %add.6), channel_id=1, source_target_pairs={{1,0},{2,1},{3,2},{4,3},{5,4},{6,5},{7,6},{8,7},{9,8},{10,9},{11,1... | collective-permute-start | bytes 3145736 | tf_op jit(solution)/shard_map/ppermute | solution.py:311
  75.4 0.0 collective-permute-done.8
  75.5 0.0 copy-done.4
  75.5 0.4 add.7
  75.9 3.9 %collective-permute-start.9 = (bf16[2,128,2048]{2,1,0:T(8,128)(2,1)S(1)}, bf16[2,128,2048]{2,1,0:T(8,128)(2,1)S(1)}, u32[]{:S(2)}, u32[]{:S(2)}) collective-permute-start(bf16[2,128,2048]{2,1,0:T(8,128)(2,1)S(1)} %add.7), channel_id=1, source_target_pairs={{0,1},{1,2},{2,3},{3,4},{4,5},{5,6},{6,7},{7,8},{8,9},{9,10},{10,1... | collective-permute-start | bytes 3145736 | tf_op jit(solution)/shard_map/ppermute | solution.py:311
  79.8 0.0 collective-permute-done.5.other_ref
  79.8 21.0 %collective-permute-done.7.above_ref = bf16[2,128,2048]{2,1,0:T(8,128)(2,1)S(1)} collective-permute-done((bf16[2,128,2048]{2,1,0:T(8,128)(2,1)S(1)}, bf16[2,128,2048]{2,1,0:T(8,128)(2,1)S(1)}, u32[]{:S(2)}, u32[]{:S(2)}) %collective-permute-start.7) | collective-permute-done | bytes 1048608 | tf_op jit(solution)/shard_map/ppermute | solution.py:311
  100.8 7.8 %collective-permute-done.9.below_ref = bf16[2,128,2048]{2,1,0:T(8,128)(2,1)S(1)} collective-permute-done((bf16[2,128,2048]{2,1,0:T(8,128)(2,1)S(1)}, bf16[2,128,2048]{2,1,0:T(8,128)(2,1)S(1)}, u32[]{:S(2)}, u32[]{:S(2)}) %collective-permute-start.9) | collective-permute-done | bytes 1048608 | tf_op jit(solution)/shard_map/ppermute | solution.py:311
  108.6 0.0 copy-done.1
  108.6 3.7 %add_up.1 = f32[4096,128]{1,0:T(8,128)} custom-call(f32[2,128,2048]{2,1,0:T(8,128)S(1)} %copy-done.1, bf16[2,128,2048]{2,1,0:T(8,128)(2,1)S(1)} %collective-permute-done.5.other_ref, bf16[2,128,2048]{2,1,0:T(8,128)(2,1)S(1)} %collective-permute-done.7.above_ref, bf16[2,128,2048]{2,1,0:T(8,128)(2,1)S(1)} %collective-permute-done.9.below_ref), custom_call_target="tpu_custom_call" | custom-call | tf_op jit(solution)/shard_map/add_up/pallas_call | solution.py:79
  (3 shorter events, 0.1 us)
Async XLA Ops:
  0.0 1.6 %copy-start.2 = (f32[1,128,2,2048]{3,2,1,0:T(2,128)S(1)}, f32[1,128,2,2048]{3,2,1,0:T(2,128)}, u32[]{:S(2)}) copy-start(f32[1,128,2,2048]{3,2,1,0:T(2,128)} %param.8) | copy-start | bytes 6291460
  1.6 40.6 %copy-start.5 = (bf16[256,2,256]{2,1,0:T(2,128)(2,1)S(1)}, bf16[256,2,256]{2,1,0:T(2,128)(2,1)}, u32[]{:S(2)}) copy-start(bf16[256,2,256]{2,1,0:T(2,128)(2,1)} %param.10) | copy-start | bytes 786436
  1.6 40.9 %copy-start.7 = (s32[1,2,5,2]{2,3,1,0:T(2,128)S(1)}, s32[1,2,5,2]{2,3,1,0:T(2,128)}, u32[]{:S(2)}) copy-start(s32[1,2,5,2]{2,3,1,0:T(2,128)} %param.11) | copy-start | bytes 244
  3.3 42.3 %copy-start = (bf16[2,128,2048]{2,1,0:T(8,128)(2,1)}, bf16[2,128,2048]{2,1,0:T(8,128)(2,1)S(1)}, u32[]{:S(2)}) copy-start(bf16[2,128,2048]{2,1,0:T(8,128)(2,1)S(1)} %split_planes.1.own_ref) | copy-start | bytes 3145732
  3.3 42.3 %copy-start.6 = (bf16[256,2,256]{2,1,0:T(2,128)(2,1)S(1)}, bf16[256,2,256]{2,1,0:T(2,128)(2,1)}, u32[]{:S(2)}) copy-start(bf16[256,2,256]{2,1,0:T(2,128)(2,1)} %param.9) | copy-start | bytes 786436
  3.3 29.2 %collective-permute-start.3 = (bf16[2,128,2048]{2,1,0:T(8,128)(2,1)S(1)}, bf16[2,128,2048]{2,1,0:T(8,128)(2,1)S(1)}, u32[]{:S(2)}, u32[]{:S(2)}) collective-permute-start(bf16[2,128,2048]{2,1,0:T(8,128)(2,1)S(1)} %split_planes.1.own_ref), channel_id=1, source_target_pairs={{1,0},{2,1},{3,2},{4,3},{5,4},{6,5},{7,6},{8,7},{9,8},{10,9},{11,1... | collective-permute-start | bytes 3145736 | tf_op jit(solution)/shard_map/ppermute | solution.py:311
  10.1 32.0 %collective-permute-start.1 = (bf16[2,128,2048]{2,1,0:T(8,128)(2,1)S(1)}, bf16[2,128,2048]{2,1,0:T(8,128)(2,1)}, u32[]{:S(2)}, u32[]{:S(2)}) collective-permute-start(bf16[2,128,2048]{2,1,0:T(8,128)(2,1)S(1)} %split_planes.1.own_ref), channel_id=1, source_target_pairs={{0,1},{1,2},{2,3},{3,4},{4,5},{5,6},{6,7},{7,8},{8,9},{9,10},{10,1... | collective-permute-start | bytes 3145736 | tf_op jit(solution)/shard_map/ppermute | solution.py:311
  12.0 34.7 %collective-permute-start = (bf16[2,128,2048]{2,1,0:T(8,128)(2,1)S(1)}, bf16[2,128,2048]{2,1,0:T(8,128)(2,1)}, u32[]{:S(2)}, u32[]{:S(2)}) collective-permute-start(bf16[2,128,2048]{2,1,0:T(8,128)(2,1)S(1)} %split_planes.1.own_ref), channel_id=1, source_target_pairs={{0,128},{128,0},{1,129},{129,1},{2,130},{130,2},{3,131},{131,3},{4... | collective-permute-start | bytes 3145736 | tf_op jit(solution)/shard_map/ppermute | solution.py:315
  32.5 13.0 %copy-start.3 = (bf16[2,128,2048]{2,1,0:T(8,128)(2,1)}, bf16[2,128,2048]{2,1,0:T(8,128)(2,1)S(1)}, u32[]{:S(2)}) copy-start(bf16[2,128,2048]{2,1,0:T(8,128)(2,1)S(1)} %collective-permute-done.3.up_ref) | copy-start | bytes 3145732
  32.5 14.2 %collective-permute-start.4 = (bf16[2,128,2048]{2,1,0:T(8,128)(2,1)S(1)}, bf16[2,128,2048]{2,1,0:T(8,128)(2,1)}, u32[]{:S(2)}, u32[]{:S(2)}) collective-permute-start(bf16[2,128,2048]{2,1,0:T(8,128)(2,1)S(1)} %collective-permute-done.3.up_ref), channel_id=1, source_target_pairs={{0,128},{128,0},{1,129},{129,1},{2,130},{130,2},{3,131},{131,3},{4... | collective-permute-start | bytes 3145736 | tf_op jit(solution)/shard_map/ppermute | solution.py:315
  42.1 4.6 %collective-permute-start.2 = (bf16[2,128,2048]{2,1,0:T(8,128)(2,1)}, bf16[2,128,2048]{2,1,0:T(8,128)(2,1)}, u32[]{:S(2)}, u32[]{:S(2)}) collective-permute-start(bf16[2,128,2048]{2,1,0:T(8,128)(2,1)} %collective-permute-done.1.low_ref), channel_id=1, source_target_pairs={{0,128},{128,0},{1,129},{129,1},{2,130},{130,2},{3,131},{131,3},{4... | collective-permute-start | bytes 3145736 | tf_op jit(solution)/shard_map/ppermute | solution.py:315
  68.7 6.8 %copy-start.4 = (bf16[2,128,2048]{2,1,0:T(8,128)(2,1)S(1)}, bf16[2,128,2048]{2,1,0:T(8,128)(2,1)}, u32[]{:S(2)}) copy-start(bf16[2,128,2048]{2,1,0:T(8,128)(2,1)} %get-tuple-element.15) | copy-start | bytes 3145732
  68.7 3.0 %collective-permute-start.6 = (bf16[2,128,2048]{2,1,0:T(8,128)(2,1)}, bf16[2,128,2048]{2,1,0:T(8,128)(2,1)S(1)}, u32[]{:S(2)}, u32[]{:S(2)}) collective-permute-start(bf16[2,128,2048]{2,1,0:T(8,128)(2,1)} %get-tuple-element.14), channel_id=1, source_target_pairs={{0,128},{128,0},{1,129},{129,1},{2,130},{130,2},{3,131},{131,3},{4... | collective-permute-start | bytes 3145736 | tf_op jit(solution)/shard_map/ppermute | solution.py:315
  69.3 6.2 %collective-permute-start.8 = (bf16[2,128,2048]{2,1,0:T(8,128)(2,1)}, bf16[2,128,2048]{2,1,0:T(8,128)(2,1)S(1)}, u32[]{:S(2)}, u32[]{:S(2)}) collective-permute-start(bf16[2,128,2048]{2,1,0:T(8,128)(2,1)} %get-tuple-element.16), channel_id=1, source_target_pairs={{0,128},{128,0},{1,129},{129,1},{2,130},{130,2},{3,131},{131,3},{4... | collective-permute-start | bytes 3145736 | tf_op jit(solution)/shard_map/ppermute | solution.py:315
  69.4 10.4 %collective-permute-start.5 = (bf16[2,128,2048]{2,1,0:T(8,128)(2,1)}, bf16[2,128,2048]{2,1,0:T(8,128)(2,1)S(1)}, u32[]{:S(2)}, u32[]{:S(2)}) collective-permute-start(bf16[2,128,2048]{2,1,0:T(8,128)(2,1)} %get-tuple-element.12), channel_id=1, source_target_pairs={{0,128},{128,0},{1,129},{129,1},{2,130},{130,2},{3,131},{131,3},{4... | collective-permute-start | bytes 3145736 | tf_op jit(solution)/shard_map/ppermute | solution.py:315
  73.4 35.3 %copy-start.1 = (f32[2,128,2048]{2,1,0:T(8,128)S(1)}, f32[2,128,2048]{2,1,0:T(8,128)}, u32[]{:S(2)}) copy-start(f32[2,128,2048]{2,1,0:T(8,128)} %get-tuple-element.11.inner_ref) | copy-start | bytes 6291460
  73.4 27.5 %collective-permute-start.7 = (bf16[2,128,2048]{2,1,0:T(8,128)(2,1)S(1)}, bf16[2,128,2048]{2,1,0:T(8,128)(2,1)S(1)}, u32[]{:S(2)}, u32[]{:S(2)}) collective-permute-start(bf16[2,128,2048]{2,1,0:T(8,128)(2,1)S(1)} %add.6), channel_id=1, source_target_pairs={{1,0},{2,1},{3,2},{4,3},{5,4},{6,5},{7,6},{8,7},{9,8},{10,9},{11,1... | collective-permute-start | bytes 3145736 | tf_op jit(solution)/shard_map/ppermute | solution.py:311
  75.9 32.8 %collective-permute-start.9 = (bf16[2,128,2048]{2,1,0:T(8,128)(2,1)S(1)}, bf16[2,128,2048]{2,1,0:T(8,128)(2,1)S(1)}, u32[]{:S(2)}, u32[]{:S(2)}) collective-permute-start(bf16[2,128,2048]{2,1,0:T(8,128)(2,1)S(1)} %add.7), channel_id=1, source_target_pairs={{0,1},{1,2},{2,3},{3,4},{4,5},{5,6},{6,7},{7,8},{8,9},{9,10},{10,1... | collective-permute-start | bytes 3145736 | tf_op jit(solution)/shard_map/ppermute | solution.py:311

commit v2 on v1

v2 whole, which is shorter than its diff:
```python
import jax
import jax.numpy as jnp
import numpy as np
from jax import lax
from jax.experimental import pallas as pl
from jax.experimental.pallas import tpu as pltpu
from jax.sharding import PartitionSpec as P

SIDE = 256
M = 128
CAP = 5
LW = 2048
LANES = 128
WIDE = SIDE + LANES
BLOCKS = LW // LANES
GROUP = 8
MIB = 1024 * 1024


def dft_planes():
    n = np.arange(SIDE)
    angles = (n[:, None] * n[None, :] % SIDE) * (2.0 * np.pi / SIDE)
    factor = 1.0 / np.sqrt(SIDE)
    return (
        (np.cos(angles) * factor).astype(jnp.bfloat16),
        (-np.sin(angles) * factor).astype(jnp.bfloat16),
    )


def real_form(xp, re, im):
    return xp.concatenate(
        [xp.concatenate([re, -im], axis=1), xp.concatenate([im, re], axis=1)], axis=0
    )


def as_lines(block):
    rows = block.shape[0]
    lines = block.reshape(rows, 2, BLOCKS, LANES).transpose(0, 2, 1, 3)
    return lines.reshape(rows, 2 * BLOCKS, LANES)


def from_lines(lines):
    rows = lines.shape[0]
    block = lines.reshape(rows, BLOCKS, 2, LANES).transpose(0, 2, 1, 3)
    return block.reshape(rows, 2, LW)


LINES = 2 * BLOCKS
PITCH = LINES + GROUP
STEPS = 4
ROWS = M // STEPS


def planes_kernel(lines_ref, planes_ref, held, sems):
    copies = [
        pltpu.make_async_copy(
            lines_ref.at[pl.ds(step * ROWS, ROWS)],
            held.reshape(M, PITCH, LANES).at[pl.ds(step * ROWS, ROWS), pl.ds(0, LINES), :],
            sems.at[step],
        )
        for step in range(STEPS)
    ]
    for copy in copies:
        copy.start()
    for step, copy in enumerate(copies):
        copy.wait()
        rows = slice(step * ROWS, (step + 1) * ROWS)
        for block in range(BLOCKS):
            for part in range(2):
                first = step * ROWS * PITCH + 2 * block + part
                cells = held[pl.ds(first, ROWS, stride=PITCH), :]
                planes_ref[part, rows, block * LANES : (block + 1) * LANES] = cells.astype(
                    jnp.bfloat16
                )


def split_planes(lines):
    return pl.pallas_call(
        planes_kernel,
        out_shape=jax.ShapeDtypeStruct((2, M, LW), jnp.bfloat16),
        in_specs=[pl.BlockSpec(memory_space=pltpu.HBM)],
        out_specs=pl.BlockSpec(memory_space=pltpu.VMEM),
        scratch_shapes=[
            pltpu.VMEM((M * PITCH, LANES), jnp.float32),
            pltpu.SemaphoreType.DMA((STEPS,)),
        ],
        compiler_params=pltpu.CompilerParams(vmem_limit_bytes=8 * MIB),
        name="split_planes",
    )(lines)


def total_kernel(inner_ref, far_ref, lines_ref, held, sems):
    copies = [
        pltpu.make_async_copy(
            held.reshape(M, PITCH, LANES).at[pl.ds(step * ROWS, ROWS), pl.ds(0, LINES), :],
            lines_ref.at[pl.ds(step * ROWS, ROWS)],
            sems.at[step],
        )
        for step in range(STEPS)
    ]
    for step, copy in enumerate(copies):
        rows = slice(step * ROWS, (step + 1) * ROWS)
        for block in range(BLOCKS):
            cols = slice(block * LANES, (block + 1) * LANES)
            for part in range(2):
                cells = inner_ref[part, rows, cols] + far_ref[part, rows, cols].astype(jnp.float32)
                first = step * ROWS * PITCH + 2 * block + part
                held[pl.ds(first, ROWS, stride=PITCH), :] = cells
        copy.start()
    for copy in copies:
        copy.wait()


def add_up(inner, far):
    return pl.pallas_call(
        total_kernel,
        out_shape=jax.ShapeDtypeStruct((M, LINES, LANES), jnp.float32),
        in_specs=[pl.BlockSpec(memory_space=pltpu.VMEM)] * 2,
        out_specs=pl.BlockSpec(memory_space=pltpu.HBM),
        scratch_shapes=[
            pltpu.VMEM((M * PITCH, LANES), jnp.float32),
            pltpu.SemaphoreType.DMA((STEPS,)),
        ],
        compiler_params=pltpu.CompilerParams(vmem_limit_bytes=12 * MIB),
        name="add_up",
    )(inner, far)


def product(a_re, a_im, b_re, b_im):
    return a_re * b_re - a_im * b_im, a_re * b_im + a_im * b_re


def conj_product(a_re, a_im, b_re, b_im):
    return a_re * b_re + a_im * b_im, a_re * b_im - a_im * b_re


def lanes(cells, count):
    return [cells[..., k * LANES : (k + 1) * LANES] for k in range(count)]


def wide(value):
    return value.astype(jnp.float32)


def probes_kernel(
    device_ref,
    places_ref,
    counts_ref,
    own_ref,
    own_o_ref,
    near_ref,
    near_o_ref,
    far_ref,
    far_o_ref,
    observed_ref,
    probe_ref,
    prop_hbm,
    dft_hbm,
    inner_out,
    inner_o_out,
    near_out,
    near_o_out,
    far_out,
    far_o_out,
    cuts,
    observed,
    window,
    object_1,
    psi_1,
    columns,
    rows,
    totals,
    matrices,
    cut_sems,
    observed_sem,
    matrix_sems,
):
    mine = device_ref[0]
    other = 1 - mine
    odd = device_ref[1]
    near_part, far_part = 2 - 2 * odd, 2 * odd

    def place(slot):
        row = places_ref[mine * CAP + slot, 0]
        col = places_ref[mine * CAP + slot, 1]
        base = pl.multiple_of(jnp.minimum(col // LANES, BLOCKS - 3) * LANES, LANES)
        row_base = pl.multiple_of(jnp.minimum(row // GROUP, M // GROUP - 1) * GROUP, GROUP)
        return row, row_base, row - row_base, base, col - base

    places = [place(slot) for slot in range(CAP)]

    def cut_copies(which, slot):
        base = places[slot][3]
        sources = ((near_ref, own_ref, far_ref), (near_o_ref, own_o_ref, far_o_ref))[which]
        return [
            pltpu.make_async_copy(
                source.at[:, :, pl.ds(base, WIDE)],
                cuts.at[(mine, other)[which], slot, part],
                cut_sems.at[which, slot, k],
            )
            for k, (part, source) in enumerate(zip((near_part, 1, far_part), sources))
        ]

    matrix_copies = [
        pltpu.make_async_copy(source, matrices.at[k], matrix_sems.at[k])
        for k, source in enumerate((prop_hbm, dft_hbm))
    ]
    for slot in range(CAP):
        for which in range(2):
            for copy in cut_copies(which, slot):
                copy.start()
        if slot == 0:
            matrix_copies[0].start()
    matrix_copies[1].start()
    prop_ref, prop_t_ref = matrices.at[0, 0], matrices.at[0, 1]
    dft_ref, dft_t_ref = matrices.at[1, 0], matrices.at[1, 1]
    observed_copy = pltpu.make_async_copy(observed_ref.at[mine], observed, observed_sem)
    observed_copy.start()
    totals[...] = jnp.zeros_like(totals)

    rim_row = lax.broadcasted_iota(jnp.int32, (M, WIDE), 0)
    lane_of_rim = lax.broadcasted_iota(jnp.int32, (M, LANES), 1)
    lane = lax.broadcasted_iota(jnp.int32, (SIDE + GROUP, LANES), 1)
    line = lax.broadcasted_iota(jnp.int32, (SIDE // GROUP, GROUP, SIDE), 1)
    line_out = lax.broadcasted_iota(jnp.int32, (1, GROUP, SIDE), 1)

    def cut(slice_no, slot, part):
        row, row_base, row_offset, _, offset = places[slot]
        back = lax.rem(LANES - offset, LANES)
        row_back = lax.rem(GROUP - row_offset, GROUP)
        keep = lane_of_rim < LANES - offset
        held = window.at[slot % 2, part]

        def to_left(cells):
            turned = [pltpu.roll(block, back, 1) for block in lanes(cells, 3)]
            return [jnp.where(keep, turned[k], turned[k + 1]) for k in range(2)]

        rim = to_left(
            jnp.where(
                rim_row >= row,
                wide(cuts[slice_no, slot, 0, part]),
                wide(cuts[slice_no, slot, 2, part]),
            )
        )
        middle = to_left(wide(cuts[slice_no, slot, 1, part]))
        for k in range(2):
            here = slice(k * LANES, (k + 1) * LANES)
            held[0:M, here] = rim[k]
            held[M : 2 * M, here] = middle[k]
            held[2 * M : 3 * M, here] = rim[k]
        cells = held[pl.ds(row_base, SIDE + GROUP), :].reshape(SIDE // GROUP + 1, GROUP, SIDE)
        cells = pltpu.roll(cells, row_back, 1)
        cells = jnp.where(line < GROUP - row_offset, cells[:-1], cells[1:])
        return cells.reshape(SIDE, SIDE)

    def add_patch(slice_no, slot, patch):
        _, row_base, row_offset, base, offset = places[slot]
        row_forth = lax.rem(row_offset, GROUP)
        forth = lax.rem(offset, LANES)
        for part in range(2):
            cells = pltpu.roll(patch[part].reshape(SIDE // GROUP, GROUP, SIDE), row_forth, 1)
            late = line_out >= row_offset
            cells = jnp.concatenate(
                [
                    jnp.where(late, cells[:1], 0.0),
                    jnp.where(line[1:] >= row_offset, cells[1:], cells[:-1]),
                    jnp.where(late, 0.0, cells[-1:]),
                ],
                axis=0,
            ).reshape(SIDE + GROUP, SIDE)
            turned = [pltpu.roll(block, forth, 1) for block in lanes(cells, 2)]
            late = lane >= offset
            spread = jnp.concatenate(
                [
                    jnp.where(late, turned[0], 0.0),
                    jnp.where(late, turned[1], turned[0]),
                    jnp.where(late, 0.0, turned[1]),
                ],
                axis=1,
            )
            totals[slice_no, part, pl.ds(row_base, SIDE + GROUP), pl.ds(base, WIDE)] += spread

    def to_columns(slot, wave, matrix):
        for part in range(2):
            columns[slot, part * SIDE : (part + 1) * SIDE, :] = wave[part].astype(jnp.bfloat16)
        middle = jnp.dot(matrix[...], columns[slot], preferred_element_type=jnp.float32)
        for part in range(2):
            rows[slot, :, part * SIDE : (part + 1) * SIDE] = middle[
                part * SIDE : (part + 1) * SIDE
            ].astype(jnp.bfloat16)

    def from_rows(slot, matrix):
        result = jnp.dot(rows[slot], matrix[...], preferred_element_type=jnp.float32)
        return result[:, :SIDE], result[:, SIDE:]

    def rounded(wave):
        return tuple(wide(plane.astype(jnp.bfloat16)) for plane in wave)

    def psi_0():
        return wide(probe_ref[0]), wide(probe_ref[1])

    def held_pair(ref, slot):
        return wide(ref[slot, 0]), wide(ref[slot, 1])

    for slot in range(CAP):
        for which in range(2):
            for copy in cut_copies(which, slot):
                copy.wait()
        phi = product(*psi_0(), cut(0, slot, 0), cut(0, slot, 1))
        if slot == 0:
            matrix_copies[0].wait()
        to_columns(slot, phi, prop_ref)
    matrix_copies[1].wait()
    for slot in range(CAP):
        for part in range(2):
            object_1[slot, part] = cut(1, slot, part).astype(jnp.bfloat16)
        wave = from_rows(slot, prop_t_ref)
        for part in range(2):
            psi_1[slot, part] = wave[part].astype(jnp.bfloat16)
        phi = product(*rounded(wave), *held_pair(object_1, slot))
        to_columns(slot, phi, dft_ref)
    observed_copy.wait()
    for slot in range(CAP):
        far_re, far_im = from_rows(slot, dft_t_ref)
        live = (slot < counts_ref[mine]).astype(jnp.float32)
        misfit = live * (far_re * far_re + far_im * far_im - observed[slot])
        to_columns(slot, (misfit * far_re, misfit * far_im), dft_t_ref)
    for slot in range(CAP):
        spread = rounded(from_rows(slot, dft_ref))
        to_columns(slot, conj_product(*held_pair(object_1, slot), *spread), prop_t_ref)
        add_patch(1, slot, conj_product(*held_pair(psi_1, slot), *spread))
    for slot in range(CAP):
        spread = rounded(from_rows(slot, prop_ref))
        add_patch(0, slot, conj_product(*psi_0(), *spread))

    def narrow(slice_no, first_row):
        return totals[slice_no, :, pl.ds(first_row, M), :].astype(jnp.bfloat16)

    near_row = pl.multiple_of(near_part * M, M)
    far_row = pl.multiple_of(far_part * M, M)
    far_o_out[...] = narrow(other, far_row)
    near_o_out[...] = narrow(other, near_row)
    far_out[...] = narrow(mine, far_row)
    near_out[...] = narrow(mine, near_row)
    inner_o_out[...] = narrow(other, M)
    inner_out[...] = totals[mine, :, M : 2 * M, :]


def probes(device, places, counts, planes, observed, probe, prop, dft):
    smem = pl.BlockSpec(memory_space=pltpu.SMEM)
    vmem = pl.BlockSpec(memory_space=pltpu.VMEM)
    apart = pl.BlockSpec(memory_space=pl.ANY)
    rim = jax.ShapeDtypeStruct((2, M, LW), jnp.bfloat16)
    return pl.pallas_call(
        probes_kernel,
        out_shape=[jax.ShapeDtypeStruct((2, M, LW), jnp.float32)] + [rim] * 5,
        in_specs=[smem] * 3 + [vmem] * 6 + [apart, vmem, apart, apart],
        out_specs=[vmem] * 6,
        scratch_shapes=[
            pltpu.VMEM((2, CAP, 3, 2, M, WIDE), jnp.bfloat16),
            pltpu.VMEM((CAP, SIDE, SIDE), jnp.float32),
            pltpu.VMEM((2, 2, 3 * M, SIDE), jnp.float32),
            pltpu.VMEM((CAP, 2, SIDE, SIDE), jnp.bfloat16),
            pltpu.VMEM((CAP, 2, SIDE, SIDE), jnp.bfloat16),
            pltpu.VMEM((CAP, 2 * SIDE, SIDE), jnp.bfloat16),
            pltpu.VMEM((CAP, SIDE, 2 * SIDE), jnp.bfloat16),
            pltpu.VMEM((2, 2, 3 * M, LW), jnp.float32),
            pltpu.VMEM((2, 2, 2 * SIDE, 2 * SIDE), jnp.bfloat16),
            pltpu.SemaphoreType.DMA((2, CAP, 3)),
            pltpu.SemaphoreType.DMA,
            pltpu.SemaphoreType.DMA((2,)),
        ],
        compiler_params=pltpu.CompilerParams(vmem_limit_bytes=38 * MIB),
        name="probes",
    )(device, places, counts, *planes, observed, probe, prop, dft)


def swap_near(value):
    count = lax.axis_size("tile")
    return lax.ppermute(value, "tile", [(t, t ^ 1) for t in range(count)])


def swap_far(value):
    count = lax.axis_size("tile")
    pairs = [(t, t + 1) for t in range(1, count - 1, 2)]
    return lax.ppermute(value, "tile", pairs + [(b, a) for a, b in pairs])


def across(value):
    return lax.ppermute(value, "depth", [(0, 1), (1, 0)])


def local(object_layer_slices, probe_wave, propagator, positions, counts, measured):
    lines = pltpu.with_memory_space_constraint(as_lines(object_layer_slices[0]), pltpu.HBM)
    own = split_planes(lines)
    near = swap_near(own)
    far = swap_far(own)
    own_o = across(own)

    device = jnp.stack([lax.axis_index("depth"), lax.axis_index("tile") % 2]).astype(jnp.int32)
    probe = jnp.stack([probe_wave[:, 0], probe_wave[:, 1]])
    prop = real_form(jnp, propagator[:, 0], propagator[:, 1])
    prop = jnp.stack([prop, prop.T])
    dft = real_form(np, *dft_planes())
    dft = jnp.asarray(np.stack([dft, dft.T]))
    near, probe, prop, places, live, device = lax.optimization_barrier(
        (near, probe, prop, positions.reshape(2 * CAP, 2), counts.reshape(2), device)
    )
    near_o = across(near)
    far_o = across(far)
    inner, inner_o, near_g, near_og, far_g, far_og = probes(
        device, places, live, (own, own_o, near, near_o, far, far_o), measured[0], probe, prop, dft
    )
    far_og = across(far_og)
    near_og = across(near_og)
    far_og, near_og, inner_o = lax.optimization_barrier((far_og, near_og, inner_o))
    far = swap_far(far_g + far_og)
    near = swap_near(near_g + near_og)
    inner = inner + across(inner_o).astype(jnp.float32)
    inner = inner + near.astype(jnp.float32)
    inner, far = lax.optimization_barrier((inner, far))
    return from_lines(add_up(inner, far))[None]


def solution(mesh):
    placed = (
        P("depth", "tile", None, None),
        P(),
        P(),
        P("tile", None, None, None),
        P("tile", None),
        P("tile", None, None, None, None),
    )
    return jax.shard_map(
        local, mesh=mesh, in_specs=placed, out_specs=P("depth", "tile", None, None), check_vma=False
    )
```

time: 113 us -> 95.6 us (0.85)
  Pallas kernels: 27.3 us -> 19.4 us
  waiting for transfers between devices: 60.8 us -> 55.1 us
  local copies, waits for them, and re-layouts: 4.49 us -> 2.92 us
  other arithmetic: 3.64 us -> 2.27 us
    ppermute x4, waiting for transfers between devices: 58.8 us -> 47.5 us  [the longest x2 39.6 us: swap_near(): return lax.ppermute(value, 'tile', [(t, t ^ 1) for t in range(count)])]
    pallas_call x1, Pallas kernels: 22 us -> 16.2 us  [probes(): pl.pallas_call(probes_kernel, out_shape=[jax.ShapeDtypeStruct((2, M, LW),...]
    ppermute x6, waiting for transfers between devices: 2 us -> 7.55 us  [across(): return lax.ppermute(value, 'depth', [(0, 1), (1, 0)])]
    pallas_call x1, Pallas kernels: 3.67 us -> 1.44 us  [add_up(): pl.pallas_call(total_kernel, out_shape=jax.ShapeDtypeStruct((M, LINES, LA...]
  transfers between devices with their start and end apart: 10 -> 10, of which waited for: 5 -> 7; matrix products, arithmetic and copies ran while one was open for 6% -> 4% of each run, Pallas kernels for 0% -> 0%
where the time goes in v2:
time: 95.6 us; the launch traced here: 95.4 us
  waiting for transfers between devices  55.1 us (58%)
  Pallas kernels  19.4 us (20%)
  starting transfers between devices  15.4 us (16%)
  local copies, waits for them, and re-layouts  2.92 us (3%)
  other arithmetic  2.27 us (2%)
    ppermute x2, waiting for transfers between devices, swap_near(): return lax.ppermute(value, 'tile', [(t, t ^ 1) for t in range(count)])  39.6 us
    pallas_call x1, Pallas kernels, probes(): pl.pallas_call(probes_kernel, out_shape=[jax.ShapeDtypeStruct((2, M, LW),...  16.2 us
    ppermute x2, starting transfers between devices, swap_far(): return lax.ppermute(value, 'tile', pairs + [(b, a) for a, b in pairs])  13.3 us
    ppermute x2, waiting for transfers between devices, swap_far(): return lax.ppermute(value, 'tile', pairs + [(b, a) for a, b in pairs])  7.91 us
    ppermute x6, waiting for transfers between devices, across(): return lax.ppermute(value, 'depth', [(0, 1), (1, 0)])  7.55 us
  transfers between devices with their start and end apart: 10, of which 7 were waited for; matrix products, arithmetic and copies ran while one was open for 4% of the time, Pallas kernels for 0%

profile of v2, /device:TPU:128, one launch (start us, length us, event | category | flops | bytes accessed | tf_op | source)
XLA Modules:
  0.0 95.4 jit_solution(2789746891853922413)
XLA Ops:
  0.0 0.0 copy-start.4
  0.0 0.0 copy-start.6
  0.0 1.7 %split_planes.1.own_ref = bf16[2,128,2048]{2,1,0:T(8,128)(2,1)S(1)} custom-call(f32[128,32,128]{2,1,0:T(8,128)} %bitcast.31), custom_call_target="tpu_custom_call" | custom-call | tf_op jit(solution)/shard_map/split_planes/pallas_call | solution.py:78
  1.7 0.0 copy-start.5
  1.7 6.8 %collective-permute-start.3 = (bf16[2,128,2048]{2,1,0:T(8,128)(2,1)S(1)}, bf16[2,128,2048]{2,1,0:T(8,128)(2,1)}, u32[]{:S(2)}, u32[]{:S(2)}) collective-permute-start(bf16[2,128,2048]{2,1,0:T(8,128)(2,1)S(1)} %split_planes.1.own_ref), channel_id=1, source_target_pairs={{1,2},{3,4},{5,6},{7,8},{9,10},{11,12},{13,14},{15,16},{17,18},{19... | collective-permute-start | bytes 3145736 | tf_op jit(solution)/shard_map/ppermute | solution.py:386
  8.5 0.1 collective-permute-start.1
  8.6 0.1 collective-permute-start
  8.7 0.0 copy-done.4
  8.7 0.4 fusion.2
  9.1 0.1 copy.20
  9.3 0.0 copy-done.6
  9.3 0.1 reshape.13
  9.4 0.1 copy.19
  9.5 0.9 fusion.1
  10.4 1.0 %copy.13 = bf16[1,512,512]{2,1,0:T(8,128)(2,1)} copy(bf16[1,512,512]{1,2,0:T(8,128)(2,1)S(1)} %get-tuple-element.39) | data formatting | bytes 1048576 | tf_op jit(solution)/shard_map/stack | solution.py:403
  11.4 0.0 copy-start.2
  11.4 0.0 copy-start.3
  11.4 0.1 pad_add_fusion.device_ref
  11.5 0.0 copy-done.5
  11.5 0.0 copy-start
  11.5 0.0 copy-start.1
  11.5 0.4 fusion.3
  11.9 0.5 copy-done.2
  12.4 0.2 copy-done.3
  12.6 0.1 pad_maximum_fusion.prop_hbm
  12.7 21.6 %collective-permute-done.near_ref = bf16[2,128,2048]{2,1,0:T(8,128)(2,1)} collective-permute-done((bf16[2,128,2048]{2,1,0:T(8,128)(2,1)S(1)}, bf16[2,128,2048]{2,1,0:T(8,128)(2,1)}, u32[]{:S(2)}, u32[]{:S(2)}) %collective-permute-start) | collective-permute-done | bytes 1048608 | tf_op jit(solution)/shard_map/ppermute | solution.py:380
  34.3 0.0 collective-permute-done.3.far_ref
  34.3 0.0 collective-permute-start.4
  34.3 0.5 collective-permute-start.2
  34.8 0.1 copy.15.places_ref
  34.9 0.0 collective-permute-done.1.own_o_ref
  34.9 2.4 %collective-permute-done.4.far_o_ref = bf16[2,128,2048]{2,1,0:T(8,128)(2,1)} collective-permute-done((bf16[2,128,2048]{2,1,0:T(8,128)(2,1)}, bf16[2,128,2048]{2,1,0:T(8,128)(2,1)}, u32[]{:S(2)}, u32[]{:S(2)}) %collective-permute-start.4) | collective-permute-done | bytes 1048608 | tf_op jit(solution)/shard_map/ppermute | solution.py:390
  37.3 1.5 %collective-permute-done.2.near_o_ref = bf16[2,128,2048]{2,1,0:T(8,128)(2,1)} collective-permute-done((bf16[2,128,2048]{2,1,0:T(8,128)(2,1)}, bf16[2,128,2048]{2,1,0:T(8,128)(2,1)}, u32[]{:S(2)}, u32[]{:S(2)}) %collective-permute-start.2) | collective-permute-done | bytes 1048608 | tf_op jit(solution)/shard_map/ppermute | solution.py:390
  38.8 0.0 copy-done
  38.8 0.0 copy-done.1
  38.8 16.2 %probes.1 = (f32[2,128,2048]{2,1,0:T(8,128)S(1)}, bf16[2,128,2048]{2,1,0:T(8,128)(2,1)S(1)}, bf16[2,128,2048]{2,1,0:T(8,128)(2,1)S(1)}, bf16[2,128,2048]{2,1,0:T...) custom-call(s32[2]{0:T(128)S(1)} %pad_add_fusion.device_ref, ...), custom_call_target="tpu_custom_call" | custom-call | tf_op jit(solution)/shard_map/probes/pallas_call | solution.py:354
  55.1 0.7 collective-permute-start.5
  55.7 0.2 collective-permute-start.6
  55.9 2.1 %collective-permute-done.5 = bf16[2,128,2048]{2,1,0:T(8,128)(2,1)S(1)} collective-permute-done((bf16[2,128,2048]{2,1,0:T(8,128)(2,1)S(1)}, bf16[2,128,2048]{2,1,0:T(8,128)(2,1)S(1)}, u32[]{:S(2)}, u32[]{:S(2)}) %collective-permute-start.5) | collective-permute-done | bytes 1048608 | tf_op jit(solution)/shard_map/ppermute | solution.py:390
  58.0 1.5 %collective-permute-done.6 = bf16[2,128,2048]{2,1,0:T(8,128)(2,1)S(1)} collective-permute-done((bf16[2,128,2048]{2,1,0:T(8,128)(2,1)S(1)}, bf16[2,128,2048]{2,1,0:T(8,128)(2,1)S(1)}, u32[]{:S(2)}, u32[]{:S(2)}) %collective-permute-start.6) | collective-permute-done | bytes 1048608 | tf_op jit(solution)/shard_map/ppermute | solution.py:390
  59.5 0.4 add.18
  59.9 0.6 collective-permute-start.8
  60.5 0.0 collective-permute-start.7
  60.5 0.4 add.20
  60.9 6.5 %collective-permute-start.9 = (bf16[2,128,2048]{2,1,0:T(8,128)(2,1)S(1)}, bf16[2,128,2048]{2,1,0:T(8,128)(2,1)S(1)}, u32[]{:S(2)}, u32[]{:S(2)}) collective-permute-start(bf16[2,128,2048]{2,1,0:T(8,128)(2,1)S(1)} %add.20), channel_id=1, source_target_pairs={{1,2},{3,4},{5,6},{7,8},{9,10},{11,12},{13,14},{15,16},{17,18},{19... | collective-permute-start | bytes 3145736 | tf_op jit(solution)/shard_map/ppermute | solution.py:386
  67.4 18.0 %collective-permute-done.8 = bf16[2,128,2048]{2,1,0:T(8,128)(2,1)S(1)} collective-permute-done((bf16[2,128,2048]{2,1,0:T(8,128)(2,1)S(1)}, bf16[2,128,2048]{2,1,0:T(8,128)(2,1)S(1)}, u32[]{:S(2)}, u32[]{:S(2)}) %collective-permute-start.8) | collective-permute-done | bytes 1048608 | tf_op jit(solution)/shard_map/ppermute | solution.py:380
  85.4 0.0 collective-permute-done.7
  85.4 0.4 convert_add_fusion.inner_ref
  85.9 7.9 %collective-permute-done.9.far_ref = bf16[2,128,2048]{2,1,0:T(8,128)(2,1)S(1)} collective-permute-done((bf16[2,128,2048]{2,1,0:T(8,128)(2,1)S(1)}, bf16[2,128,2048]{2,1,0:T(8,128)(2,1)S(1)}, u32[]{:S(2)}, u32[]{:S(2)}) %collective-permute-start.9) | collective-permute-done | bytes 1048608 | tf_op jit(solution)/shard_map/ppermute | solution.py:386
  93.8 1.4 %add_up.1 = f32[128,32,128]{2,1,0:T(8,128)} custom-call(f32[2,128,2048]{2,1,0:T(8,128)S(1)} %convert_add_fusion.inner_ref, bf16[2,128,2048]{2,1,0:T(8,128)(2,1)S(1)} %collective-permute-done.9.far_ref), custom_call_target="tpu_custom_call" | custom-call | tf_op jit(solution)/shard_map/add_up/pallas_call | solution.py:115
  (4 shorter events, 0.1 us)
Async XLA Ops:
  0.0 8.7 %copy-start.4 = (bf16[256,2,256]{2,1,0:T(2,128)(2,1)S(1)}, bf16[256,2,256]{2,1,0:T(2,128)(2,1)}, u32[]{:S(2)}) copy-start(bf16[256,2,256]{2,1,0:T(2,128)(2,1)} %param.9) | copy-start | bytes 786436
  0.0 9.3 %copy-start.6 = (s32[1,2,5,2]{2,3,1,0:T(2,128)S(1)}, s32[1,2,5,2]{2,3,1,0:T(2,128)}, u32[]{:S(2)}) copy-start(s32[1,2,5,2]{2,3,1,0:T(2,128)} %param.10) | copy-start | bytes 244
  1.7 9.8 %copy-start.5 = (bf16[256,2,256]{2,1,0:T(2,128)(2,1)S(1)}, bf16[256,2,256]{2,1,0:T(2,128)(2,1)}, u32[]{:S(2)}) copy-start(bf16[256,2,256]{2,1,0:T(2,128)(2,1)} %param.8) | copy-start | bytes 786436
  1.7 32.6 %collective-permute-start.3 = (bf16[2,128,2048]{2,1,0:T(8,128)(2,1)S(1)}, bf16[2,128,2048]{2,1,0:T(8,128)(2,1)}, u32[]{:S(2)}, u32[]{:S(2)}) collective-permute-start(bf16[2,128,2048]{2,1,0:T(8,128)(2,1)S(1)} %split_planes.1.own_ref), channel_id=1, source_target_pairs={{1,2},{3,4},{5,6},{7,8},{9,10},{11,12},{13,14},{15,16},{17,18},{19... | collective-permute-start | bytes 3145736 | tf_op jit(solution)/shard_map/ppermute | solution.py:386
  8.5 26.4 %collective-permute-start.1 = (bf16[2,128,2048]{2,1,0:T(8,128)(2,1)S(1)}, bf16[2,128,2048]{2,1,0:T(8,128)(2,1)}, u32[]{:S(2)}, u32[]{:S(2)}) collective-permute-start(bf16[2,128,2048]{2,1,0:T(8,128)(2,1)S(1)} %split_planes.1.own_ref), channel_id=1, source_target_pairs={{0,128},{128,0},{1,129},{129,1},{2,130},{130,2},{3,131},{131,3},{4... | collective-permute-start | bytes 3145736 | tf_op jit(solution)/shard_map/ppermute | solution.py:390
  8.6 25.7 %collective-permute-start = (bf16[2,128,2048]{2,1,0:T(8,128)(2,1)S(1)}, bf16[2,128,2048]{2,1,0:T(8,128)(2,1)}, u32[]{:S(2)}, u32[]{:S(2)}) collective-permute-start(bf16[2,128,2048]{2,1,0:T(8,128)(2,1)S(1)} %split_planes.1.own_ref), channel_id=1, source_target_pairs={{0,1},{1,0},{2,3},{3,2},{4,5},{5,4},{6,7},{7,6},{8,9},{9,8},{10,11... | collective-permute-start | bytes 3145736 | tf_op jit(solution)/shard_map/ppermute | solution.py:380
  11.4 1.0 %copy-start.2 = (bf16[1,512,512]{2,1,0:T(8,128)(2,1)S(1)}, bf16[1,512,512]{2,1,0:T(8,128)(2,1)}, u32[]{:S(2)}) copy-start(bf16[1,512,512]{2,1,0:T(8,128)(2,1)} %copy.13) | copy-start | bytes 1572868
  11.4 1.2 %copy-start.3 = (bf16[1,512,512]{2,1,0:T(8,128)(2,1)S(1)}, bf16[1,512,512]{2,1,0:T(8,128)(2,1)}, u32[]{:S(2)}) copy-start(bf16[1,512,512]{2,1,0:T(8,128)(2,1)} %get-tuple-element.40) | copy-start | bytes 1572868
  11.5 27.3 %copy-start = (bf16[2,512,512]{2,1,0:T(8,128)(2,1)S(1)}, bf16[2,512,512]{2,1,0:T(8,128)(2,1)}, u32[]{:S(2)}) copy-start(bf16[2,512,512]{2,1,0:T(8,128)(2,1)} %constant.24.clone.dft_hbm) | copy-start | bytes 3145732
  11.5 27.3 %copy-start.1 = (s32[1,2]{1,0:T(1,128)S(1)}, s32[1,2]{1,0:T(1,128)}, u32[]{:S(2)}) copy-start(s32[1,2]{1,0:T(1,128)} %param.11) | copy-start | bytes 28
  34.3 3.0 %collective-permute-start.4 = (bf16[2,128,2048]{2,1,0:T(8,128)(2,1)}, bf16[2,128,2048]{2,1,0:T(8,128)(2,1)}, u32[]{:S(2)}, u32[]{:S(2)}) collective-permute-start(bf16[2,128,2048]{2,1,0:T(8,128)(2,1)} %collective-permute-done.3.far_ref), channel_id=1, source_target_pairs={{0,128},{128,0},{1,129},{129,1},{2,130},{130,2},{3,131},{131,3},{4... | collective-permute-start | bytes 3145736 | tf_op jit(solution)/shard_map/ppermute | solution.py:390
  34.3 4.5 %collective-permute-start.2 = (bf16[2,128,2048]{2,1,0:T(8,128)(2,1)}, bf16[2,128,2048]{2,1,0:T(8,128)(2,1)}, u32[]{:S(2)}, u32[]{:S(2)}) collective-permute-start(bf16[2,128,2048]{2,1,0:T(8,128)(2,1)} %collective-permute-done.near_ref), channel_id=1, source_target_pairs={{0,128},{128,0},{1,129},{129,1},{2,130},{130,2},{3,131},{131,3},{4... | collective-permute-start | bytes 3145736 | tf_op jit(solution)/shard_map/ppermute | solution.py:390
  55.1 3.0 %collective-permute-start.5 = (bf16[2,128,2048]{2,1,0:T(8,128)(2,1)S(1)}, bf16[2,128,2048]{2,1,0:T(8,128)(2,1)S(1)}, u32[]{:S(2)}, u32[]{:S(2)}) collective-permute-start(bf16[2,128,2048]{2,1,0:T(8,128)(2,1)S(1)} %get-tuple-element.29), channel_id=1, source_target_pairs={{0,128},{128,0},{1,129},{129,1},{2,130},{130,2},{3,131},{131,3},{4... | collective-permute-start | bytes 3145736 | tf_op jit(solution)/shard_map/ppermute | solution.py:390
  55.7 3.8 %collective-permute-start.6 = (bf16[2,128,2048]{2,1,0:T(8,128)(2,1)S(1)}, bf16[2,128,2048]{2,1,0:T(8,128)(2,1)S(1)}, u32[]{:S(2)}, u32[]{:S(2)}) collective-permute-start(bf16[2,128,2048]{2,1,0:T(8,128)(2,1)S(1)} %get-tuple-element.30), channel_id=1, source_target_pairs={{0,128},{128,0},{1,129},{129,1},{2,130},{130,2},{3,131},{131,3},{4... | collective-permute-start | bytes 3145736 | tf_op jit(solution)/shard_map/ppermute | solution.py:390
  59.9 25.5 %collective-permute-start.8 = (bf16[2,128,2048]{2,1,0:T(8,128)(2,1)S(1)}, bf16[2,128,2048]{2,1,0:T(8,128)(2,1)S(1)}, u32[]{:S(2)}, u32[]{:S(2)}) collective-permute-start(bf16[2,128,2048]{2,1,0:T(8,128)(2,1)S(1)} %add.18), channel_id=1, source_target_pairs={{0,1},{1,0},{2,3},{3,2},{4,5},{5,4},{6,7},{7,6},{8,9},{9,8},{10,11... | collective-permute-start | bytes 3145736 | tf_op jit(solution)/shard_map/ppermute | solution.py:380
  60.5 24.9 %collective-permute-start.7 = (bf16[2,128,2048]{2,1,0:T(8,128)(2,1)S(1)}, bf16[2,128,2048]{2,1,0:T(8,128)(2,1)S(1)}, u32[]{:S(2)}, u32[]{:S(2)}) collective-permute-start(bf16[2,128,2048]{2,1,0:T(8,128)(2,1)S(1)} %get-tuple-element.32), channel_id=1, source_target_pairs={{0,128},{128,0},{1,129},{129,1},{2,130},{130,2},{3,131},{131,3},{4... | collective-permute-start | bytes 3145736 | tf_op jit(solution)/shard_map/ppermute | solution.py:390
  60.9 32.9 %collective-permute-start.9 = (bf16[2,128,2048]{2,1,0:T(8,128)(2,1)S(1)}, bf16[2,128,2048]{2,1,0:T(8,128)(2,1)S(1)}, u32[]{:S(2)}, u32[]{:S(2)}) collective-permute-start(bf16[2,128,2048]{2,1,0:T(8,128)(2,1)S(1)} %add.20), channel_id=1, source_target_pairs={{1,2},{3,4},{5,6},{7,8},{9,10},{11,12},{13,14},{15,16},{17,18},{19... | collective-permute-start | bytes 3145736 | tf_op jit(solution)/shard_map/ppermute | solution.py:386

commit v3 on v2

--- a/solution.py
+++ b/solution.py
@@ -170,6 +170,7 @@
     columns,
     rows,
     totals,
+    waves,
     matrices,
     cut_sems,
     observed_sem,
@@ -282,16 +283,23 @@
 
     def to_columns(slot, wave, matrix):
         for part in range(2):
-            columns[slot, part * SIDE : (part + 1) * SIDE, :] = wave[part].astype(jnp.bfloat16)
-        middle = jnp.dot(matrix[...], columns[slot], preferred_element_type=jnp.float32)
-        for part in range(2):
-            rows[slot, :, part * SIDE : (part + 1) * SIDE] = middle[
-                part * SIDE : (part + 1) * SIDE
-            ].astype(jnp.bfloat16)
-
-    def from_rows(slot, matrix):
-        result = jnp.dot(rows[slot], matrix[...], preferred_element_type=jnp.float32)
-        return result[:, :SIDE], result[:, SIDE:]
+            columns[part * SIDE : (part + 1) * SIDE, slot * SIDE : (slot + 1) * SIDE] = wave[part].astype(jnp.bfloat16)
+        if slot < CAP - 1:
+            return
+        middle = jnp.dot(matrix[...], columns[...], preferred_element_type=jnp.float32)
+        for k in range(CAP):
+            for part in range(2):
+                rows[k, :, part * SIDE : (part + 1) * SIDE] = middle[
+                    part * SIDE : (part + 1) * SIDE, k * SIDE : (k + 1) * SIDE
+                ].astype(jnp.bfloat16)
+
+    def all_rows(matrix):
+        every = rows[...].reshape(CAP * SIDE, 2 * SIDE)
+        result = jnp.dot(every, matrix[...], preferred_element_type=jnp.float32)
+        waves[...] = result.reshape(CAP, SIDE, 2 * SIDE)
+
+    def from_rows(slot):
+        return waves[slot, :, :SIDE], waves[slot, :, SIDE:]
 
     def rounded(wave):
         return tuple(wide(plane.astype(jnp.bfloat16)) for plane in wave)
@@ -311,26 +319,30 @@
             matrix_copies[0].wait()
         to_columns(slot, phi, prop_ref)
     matrix_copies[1].wait()
+    all_rows(prop_t_ref)
     for slot in range(CAP):
         for part in range(2):
             object_1[slot, part] = cut(1, slot, part).astype(jnp.bfloat16)
-        wave = from_rows(slot, prop_t_ref)
+        wave = from_rows(slot)
         for part in range(2):
             psi_1[slot, part] = wave[part].astype(jnp.bfloat16)
         phi = product(*rounded(wave), *held_pair(object_1, slot))
         to_columns(slot, phi, dft_ref)
     observed_copy.wait()
-    for slot in range(CAP):
-        far_re, far_im = from_rows(slot, dft_t_ref)
+    all_rows(dft_t_ref)
+    for slot in range(CAP):
+        far_re, far_im = from_rows(slot)
         live = (slot < counts_ref[mine]).astype(jnp.float32)
         misfit = live * (far_re * far_re + far_im * far_im - observed[slot])
         to_columns(slot, (misfit * far_re, misfit * far_im), dft_t_ref)
-    for slot in range(CAP):
-        spread = rounded(from_rows(slot, dft_ref))
+    all_rows(dft_ref)
+    for slot in range(CAP):
+        spread = rounded(from_rows(slot))
         to_columns(slot, conj_product(*held_pair(object_1, slot), *spread), prop_t_ref)
         add_patch(1, slot, conj_product(*held_pair(psi_1, slot), *spread))
-    for slot in range(CAP):
-        spread = rounded(from_rows(slot, prop_ref))
+    all_rows(prop_ref)
+    for slot in range(CAP):
+        spread = rounded(from_rows(slot))
         add_patch(0, slot, conj_product(*psi_0(), *spread))
 
     def narrow(slice_no, first_row):
@@ -362,9 +374,10 @@
             pltpu.VMEM((2, 2, 3 * M, SIDE), jnp.float32),
             pltpu.VMEM((CAP, 2, SIDE, SIDE), jnp.bfloat16),
             pltpu.VMEM((CAP, 2, SIDE, SIDE), jnp.bfloat16),
-            pltpu.VMEM((CAP, 2 * SIDE, SIDE), jnp.bfloat16),
+            pltpu.VMEM((2 * SIDE, CAP * SIDE), jnp.bfloat16),
             pltpu.VMEM((CAP, SIDE, 2 * SIDE), jnp.bfloat16),
             pltpu.VMEM((2, 2, 3 * M, LW), jnp.float32),
+            pltpu.VMEM((CAP, SIDE, 2 * SIDE), jnp.float32),
             pltpu.VMEM((2, 2, 2 * SIDE, 2 * SIDE), jnp.bfloat16),
             pltpu.SemaphoreType.DMA((2, CAP, 3)),
             pltpu.SemaphoreType.DMA,
@@ -413,13 +426,14 @@
     )
     far_og = across(far_og)
     near_og = across(near_og)
-    far_og, near_og, inner_o = lax.optimization_barrier((far_og, near_og, inner_o))
-    far = swap_far(far_g + far_og)
+    far_g = far_g + far_og
+    far = swap_far(far_g)
+    far_g, near_og, inner_o = lax.optimization_barrier((far_g, near_og, inner_o))
     near = swap_near(near_g + near_og)
     inner = inner + across(inner_o).astype(jnp.float32)
-    inner = inner + near.astype(jnp.float32)
-    inner, far = lax.optimization_barrier((inner, far))
-    return from_lines(add_up(inner, far))[None]
+    inner = inner + far.astype(jnp.float32)
+    inner, near = lax.optimization_barrier((inner, near))
+    return from_lines(add_up(inner, near))[None]
 
 
 def solution(mesh):

time: 95.6 us -> 92.6 us (0.969)
  waiting for transfers between devices: 55.1 us -> 53.1 us
    ppermute x2, waiting for transfers between devices: 39.6 us -> 21.6 us  [swap_near(): return lax.ppermute(value, 'tile', [(t, t ^ 1) for t in range(count)])]
    ppermute x2, waiting for transfers between devices: 7.91 us -> 25.4 us  [swap_far(): return lax.ppermute(value, 'tile', pairs + [(b, a) for a, b in pairs])]
    ppermute x6, waiting for transfers between devices: 7.55 us -> 6.05 us  [across(): return lax.ppermute(value, 'depth', [(0, 1), (1, 0)])]
  transfers between devices with their start and end apart: 10 -> 10, of which waited for: 7 -> 5; matrix products, arithmetic and copies ran while one was open for 4% -> 5% of each run, Pallas kernels for 0% -> 0%
where the time goes in v3:
time: 92.6 us; the launch traced here: 92.4 us
  waiting for transfers between devices  53.1 us (57%)
  Pallas kernels  18.9 us (20%)
  starting transfers between devices  14.8 us (16%)
  local copies, waits for them, and re-layouts  2.92 us (3%)
  other arithmetic  2.26 us (2%)
    ppermute x2, waiting for transfers between devices, swap_far(): return lax.ppermute(value, 'tile', pairs + [(b, a) for a, b in pairs])  25.4 us
    ppermute x2, waiting for transfers between devices, swap_near(): return lax.ppermute(value, 'tile', [(t, t ^ 1) for t in range(count)])  21.6 us
    pallas_call x1, Pallas kernels, probes(): pl.pallas_call(probes_kernel, out_shape=[jax.ShapeDtypeStruct((2, M, LW),...  15.8 us
    ppermute x2, starting transfers between devices, swap_far(): return lax.ppermute(value, 'tile', pairs + [(b, a) for a, b in pairs])  13.3 us
    ppermute x6, waiting for transfers between devices, across(): return lax.ppermute(value, 'depth', [(0, 1), (1, 0)])  6.05 us
  transfers between devices with their start and end apart: 10, of which 5 were waited for; matrix products, arithmetic and copies ran while one was open for 5% of the time, Pallas kernels for 0%

profile of v3, /device:TPU:128, one launch (start us, length us, event | category | flops | bytes accessed | tf_op | source)
XLA Modules:
  0.0 92.4 jit_solution(8158314740122047184)
XLA Ops:
  0.0 0.0 copy-start.4
  0.0 0.0 copy-start.6
  0.0 1.7 %split_planes.1.own_ref = bf16[2,128,2048]{2,1,0:T(8,128)(2,1)S(1)} custom-call(f32[128,32,128]{2,1,0:T(8,128)} %bitcast.31), custom_call_target="tpu_custom_call" | custom-call | tf_op jit(solution)/shard_map/split_planes/pallas_call | solution.py:78
  1.7 0.0 copy-start.5
  1.7 6.8 %collective-permute-start.3 = (bf16[2,128,2048]{2,1,0:T(8,128)(2,1)S(1)}, bf16[2,128,2048]{2,1,0:T(8,128)(2,1)}, u32[]{:S(2)}, u32[]{:S(2)}) collective-permute-start(bf16[2,128,2048]{2,1,0:T(8,128)(2,1)S(1)} %split_planes.1.own_ref), channel_id=1, source_target_pairs={{1,2},{3,4},{5,6},{7,8},{9,10},{11,12},{13,14},{15,16},{17,18},{19... | collective-permute-start | bytes 3145736 | tf_op jit(solution)/shard_map/ppermute | solution.py:399
  8.5 0.1 collective-permute-start.1
  8.6 0.1 collective-permute-start
  8.7 0.0 copy-done.4
  8.7 0.4 fusion.2
  9.1 0.1 copy.20
  9.3 0.0 copy-done.6
  9.3 0.1 reshape.13
  9.4 0.1 copy.19
  9.5 0.9 fusion.1
  10.4 1.0 %copy.13 = bf16[1,512,512]{2,1,0:T(8,128)(2,1)} copy(bf16[1,512,512]{1,2,0:T(8,128)(2,1)S(1)} %get-tuple-element.37) | data formatting | bytes 1048576 | tf_op jit(solution)/shard_map/stack | solution.py:416
  11.4 0.0 copy-start.2
  11.4 0.0 copy-start.3
  11.4 0.1 pad_add_fusion.device_ref
  11.5 0.0 copy-done.5
  11.5 0.0 copy-start
  11.5 0.0 copy-start.1
  11.5 0.4 fusion.3
  11.9 0.5 copy-done.2
  12.4 0.2 copy-done.3
  12.6 0.1 pad_maximum_fusion.prop_hbm
  12.7 21.6 %collective-permute-done.near_ref = bf16[2,128,2048]{2,1,0:T(8,128)(2,1)} collective-permute-done((bf16[2,128,2048]{2,1,0:T(8,128)(2,1)S(1)}, bf16[2,128,2048]{2,1,0:T(8,128)(2,1)}, u32[]{:S(2)}, u32[]{:S(2)}) %collective-permute-start) | collective-permute-done | bytes 1048608 | tf_op jit(solution)/shard_map/ppermute | solution.py:393
  34.3 0.0 collective-permute-done.3.far_ref
  34.3 0.0 collective-permute-start.4
  34.3 0.5 collective-permute-start.2
  34.8 0.1 copy.15.places_ref
  34.9 0.0 collective-permute-done.1.own_o_ref
  34.9 2.4 %collective-permute-done.4.far_o_ref = bf16[2,128,2048]{2,1,0:T(8,128)(2,1)} collective-permute-done((bf16[2,128,2048]{2,1,0:T(8,128)(2,1)}, bf16[2,128,2048]{2,1,0:T(8,128)(2,1)}, u32[]{:S(2)}, u32[]{:S(2)}) %collective-permute-start.4) | collective-permute-done | bytes 1048608 | tf_op jit(solution)/shard_map/ppermute | solution.py:403
  37.3 1.5 %collective-permute-done.2.near_o_ref = bf16[2,128,2048]{2,1,0:T(8,128)(2,1)} collective-permute-done((bf16[2,128,2048]{2,1,0:T(8,128)(2,1)}, bf16[2,128,2048]{2,1,0:T(8,128)(2,1)}, u32[]{:S(2)}, u32[]{:S(2)}) %collective-permute-start.2) | collective-permute-done | bytes 1048608 | tf_op jit(solution)/shard_map/ppermute | solution.py:403
  38.8 0.0 copy-done
  38.8 0.0 copy-done.1
  38.8 15.8 %probes.1 = (f32[2,128,2048]{2,1,0:T(8,128)S(1)}, bf16[2,128,2048]{2,1,0:T(8,128)(2,1)S(1)}, bf16[2,128,2048]{2,1,0:T(8,128)(2,1)S(1)}, bf16[2,128,2048]{2,1,0:T...) custom-call(s32[2]{0:T(128)S(1)} %pad_add_fusion.device_ref, ...), custom_call_target="tpu_custom_call" | custom-call | tf_op jit(solution)/shard_map/probes/pallas_call | solution.py:366
  54.6 0.3 collective-permute-start.5
  54.9 0.3 collective-permute-start.6
  55.2 2.1 %collective-permute-done.5 = bf16[2,128,2048]{2,1,0:T(8,128)(2,1)S(1)} collective-permute-done((bf16[2,128,2048]{2,1,0:T(8,128)(2,1)S(1)}, bf16[2,128,2048]{2,1,0:T(8,128)(2,1)S(1)}, u32[]{:S(2)}, u32[]{:S(2)}) %collective-permute-start.5) | collective-permute-done | bytes 1048608 | tf_op jit(solution)/shard_map/ppermute | solution.py:403
  57.4 0.4 add.17
  57.7 6.5 %collective-permute-start.8 = (bf16[2,128,2048]{2,1,0:T(8,128)(2,1)S(1)}, bf16[2,128,2048]{2,1,0:T(8,128)(2,1)S(1)}, u32[]{:S(2)}, u32[]{:S(2)}) collective-permute-start(bf16[2,128,2048]{2,1,0:T(8,128)(2,1)S(1)} %add.17), channel_id=1, source_target_pairs={{1,2},{3,4},{5,6},{7,8},{9,10},{11,12},{13,14},{15,16},{17,18},{19... | collective-permute-start | bytes 3145736 | tf_op jit(solution)/shard_map/ppermute | solution.py:399
  64.3 0.0 collective-permute-done.6
  64.3 0.1 collective-permute-start.7
  64.4 0.4 add.20
  64.8 0.1 collective-permute-start.9
  64.9 25.4 %collective-permute-done.8 = bf16[2,128,2048]{2,1,0:T(8,128)(2,1)S(1)} collective-permute-done((bf16[2,128,2048]{2,1,0:T(8,128)(2,1)S(1)}, bf16[2,128,2048]{2,1,0:T(8,128)(2,1)S(1)}, u32[]{:S(2)}, u32[]{:S(2)}) %collective-permute-start.8) | collective-permute-done | bytes 1048608 | tf_op jit(solution)/shard_map/ppermute | solution.py:399
  90.3 0.0 collective-permute-done.7
  90.3 0.4 convert_add_fusion.inner_ref
  90.7 0.0 collective-permute-done.9.far_ref
  90.7 1.4 %add_up.1 = f32[128,32,128]{2,1,0:T(8,128)} custom-call(f32[2,128,2048]{2,1,0:T(8,128)S(1)} %convert_add_fusion.inner_ref, bf16[2,128,2048]{2,1,0:T(8,128)(2,1)S(1)} %collective-permute-done.9.far_ref), custom_call_target="tpu_custom_call" | custom-call | tf_op jit(solution)/shard_map/add_up/pallas_call | solution.py:115
  (4 shorter events, 0.1 us)
Async XLA Ops:
  0.0 8.7 %copy-start.4 = (bf16[256,2,256]{2,1,0:T(2,128)(2,1)S(1)}, bf16[256,2,256]{2,1,0:T(2,128)(2,1)}, u32[]{:S(2)}) copy-start(bf16[256,2,256]{2,1,0:T(2,128)(2,1)} %param.9) | copy-start | bytes 786436
  0.0 9.3 %copy-start.6 = (s32[1,2,5,2]{2,3,1,0:T(2,128)S(1)}, s32[1,2,5,2]{2,3,1,0:T(2,128)}, u32[]{:S(2)}) copy-start(s32[1,2,5,2]{2,3,1,0:T(2,128)} %param.10) | copy-start | bytes 244
  1.7 9.8 %copy-start.5 = (bf16[256,2,256]{2,1,0:T(2,128)(2,1)S(1)}, bf16[256,2,256]{2,1,0:T(2,128)(2,1)}, u32[]{:S(2)}) copy-start(bf16[256,2,256]{2,1,0:T(2,128)(2,1)} %param.8) | copy-start | bytes 786436
  1.7 32.6 %collective-permute-start.3 = (bf16[2,128,2048]{2,1,0:T(8,128)(2,1)S(1)}, bf16[2,128,2048]{2,1,0:T(8,128)(2,1)}, u32[]{:S(2)}, u32[]{:S(2)}) collective-permute-start(bf16[2,128,2048]{2,1,0:T(8,128)(2,1)S(1)} %split_planes.1.own_ref), channel_id=1, source_target_pairs={{1,2},{3,4},{5,6},{7,8},{9,10},{11,12},{13,14},{15,16},{17,18},{19... | collective-permute-start | bytes 3145736 | tf_op jit(solution)/shard_map/ppermute | solution.py:399
  8.5 26.4 %collective-permute-start.1 = (bf16[2,128,2048]{2,1,0:T(8,128)(2,1)S(1)}, bf16[2,128,2048]{2,1,0:T(8,128)(2,1)}, u32[]{:S(2)}, u32[]{:S(2)}) collective-permute-start(bf16[2,128,2048]{2,1,0:T(8,128)(2,1)S(1)} %split_planes.1.own_ref), channel_id=1, source_target_pairs={{0,128},{128,0},{1,129},{129,1},{2,130},{130,2},{3,131},{131,3},{4... | collective-permute-start | bytes 3145736 | tf_op jit(solution)/shard_map/ppermute | solution.py:403
  8.6 25.7 %collective-permute-start = (bf16[2,128,2048]{2,1,0:T(8,128)(2,1)S(1)}, bf16[2,128,2048]{2,1,0:T(8,128)(2,1)}, u32[]{:S(2)}, u32[]{:S(2)}) collective-permute-start(bf16[2,128,2048]{2,1,0:T(8,128)(2,1)S(1)} %split_planes.1.own_ref), channel_id=1, source_target_pairs={{0,1},{1,0},{2,3},{3,2},{4,5},{5,4},{6,7},{7,6},{8,9},{9,8},{10,11... | collective-permute-start | bytes 3145736 | tf_op jit(solution)/shard_map/ppermute | solution.py:393
  11.4 1.0 %copy-start.2 = (bf16[1,512,512]{2,1,0:T(8,128)(2,1)S(1)}, bf16[1,512,512]{2,1,0:T(8,128)(2,1)}, u32[]{:S(2)}) copy-start(bf16[1,512,512]{2,1,0:T(8,128)(2,1)} %copy.13) | copy-start | bytes 1572868
  11.4 1.2 %copy-start.3 = (bf16[1,512,512]{2,1,0:T(8,128)(2,1)S(1)}, bf16[1,512,512]{2,1,0:T(8,128)(2,1)}, u32[]{:S(2)}) copy-start(bf16[1,512,512]{2,1,0:T(8,128)(2,1)} %get-tuple-element.38) | copy-start | bytes 1572868
  11.5 27.3 %copy-start = (bf16[2,512,512]{2,1,0:T(8,128)(2,1)S(1)}, bf16[2,512,512]{2,1,0:T(8,128)(2,1)}, u32[]{:S(2)}) copy-start(bf16[2,512,512]{2,1,0:T(8,128)(2,1)} %constant.24.clone.dft_hbm) | copy-start | bytes 3145732
  11.5 27.3 %copy-start.1 = (s32[1,2]{1,0:T(1,128)S(1)}, s32[1,2]{1,0:T(1,128)}, u32[]{:S(2)}) copy-start(s32[1,2]{1,0:T(1,128)} %param.11) | copy-start | bytes 28
  34.3 3.0 %collective-permute-start.4 = (bf16[2,128,2048]{2,1,0:T(8,128)(2,1)}, bf16[2,128,2048]{2,1,0:T(8,128)(2,1)}, u32[]{:S(2)}, u32[]{:S(2)}) collective-permute-start(bf16[2,128,2048]{2,1,0:T(8,128)(2,1)} %collective-permute-done.3.far_ref), channel_id=1, source_target_pairs={{0,128},{128,0},{1,129},{129,1},{2,130},{130,2},{3,131},{131,3},{4... | collective-permute-start | bytes 3145736 | tf_op jit(solution)/shard_map/ppermute | solution.py:403
  34.3 4.5 %collective-permute-start.2 = (bf16[2,128,2048]{2,1,0:T(8,128)(2,1)}, bf16[2,128,2048]{2,1,0:T(8,128)(2,1)}, u32[]{:S(2)}, u32[]{:S(2)}) collective-permute-start(bf16[2,128,2048]{2,1,0:T(8,128)(2,1)} %collective-permute-done.near_ref), channel_id=1, source_target_pairs={{0,128},{128,0},{1,129},{129,1},{2,130},{130,2},{3,131},{131,3},{4... | collective-permute-start | bytes 3145736 | tf_op jit(solution)/shard_map/ppermute | solution.py:403
  54.6 2.7 %collective-permute-start.5 = (bf16[2,128,2048]{2,1,0:T(8,128)(2,1)S(1)}, bf16[2,128,2048]{2,1,0:T(8,128)(2,1)S(1)}, u32[]{:S(2)}, u32[]{:S(2)}) collective-permute-start(bf16[2,128,2048]{2,1,0:T(8,128)(2,1)S(1)} %get-tuple-element.29), channel_id=1, source_target_pairs={{0,128},{128,0},{1,129},{129,1},{2,130},{130,2},{3,131},{131,3},{4... | collective-permute-start | bytes 3145736 | tf_op jit(solution)/shard_map/ppermute | solution.py:403
  54.9 9.4 %collective-permute-start.6 = (bf16[2,128,2048]{2,1,0:T(8,128)(2,1)S(1)}, bf16[2,128,2048]{2,1,0:T(8,128)(2,1)S(1)}, u32[]{:S(2)}, u32[]{:S(2)}) collective-permute-start(bf16[2,128,2048]{2,1,0:T(8,128)(2,1)S(1)} %get-tuple-element.30), channel_id=1, source_target_pairs={{0,128},{128,0},{1,129},{129,1},{2,130},{130,2},{3,131},{131,3},{4... | collective-permute-start | bytes 3145736 | tf_op jit(solution)/shard_map/ppermute | solution.py:403
  57.7 32.6 %collective-permute-start.8 = (bf16[2,128,2048]{2,1,0:T(8,128)(2,1)S(1)}, bf16[2,128,2048]{2,1,0:T(8,128)(2,1)S(1)}, u32[]{:S(2)}, u32[]{:S(2)}) collective-permute-start(bf16[2,128,2048]{2,1,0:T(8,128)(2,1)S(1)} %add.17), channel_id=1, source_target_pairs={{1,2},{3,4},{5,6},{7,8},{9,10},{11,12},{13,14},{15,16},{17,18},{19... | collective-permute-start | bytes 3145736 | tf_op jit(solution)/shard_map/ppermute | solution.py:399
  64.3 26.0 %collective-permute-start.7 = (bf16[2,128,2048]{2,1,0:T(8,128)(2,1)S(1)}, bf16[2,128,2048]{2,1,0:T(8,128)(2,1)S(1)}, u32[]{:S(2)}, u32[]{:S(2)}) collective-permute-start(bf16[2,128,2048]{2,1,0:T(8,128)(2,1)S(1)} %get-tuple-element.32), channel_id=1, source_target_pairs={{0,128},{128,0},{1,129},{129,1},{2,130},{130,2},{3,131},{131,3},{4... | collective-permute-start | bytes 3145736 | tf_op jit(solution)/shard_map/ppermute | solution.py:403
  64.8 25.9 %collective-permute-start.9 = (bf16[2,128,2048]{2,1,0:T(8,128)(2,1)S(1)}, bf16[2,128,2048]{2,1,0:T(8,128)(2,1)S(1)}, u32[]{:S(2)}, u32[]{:S(2)}) collective-permute-start(bf16[2,128,2048]{2,1,0:T(8,128)(2,1)S(1)} %add.20), channel_id=1, source_target_pairs={{0,1},{1,0},{2,3},{3,2},{4,5},{5,4},{6,7},{7,6},{8,9},{9,8},{10,11... | collective-permute-start | bytes 3145736 | tf_op jit(solution)/shard_map/ppermute | solution.py:393

commit v4 on v3

--- a/solution.py
+++ b/solution.py
@@ -170,7 +170,6 @@
     columns,
     rows,
     totals,
-    waves,
     matrices,
     cut_sems,
     observed_sem,
@@ -237,10 +236,12 @@
             return [jnp.where(keep, turned[k], turned[k + 1]) for k in range(2)]
 
         rim = to_left(
-            jnp.where(
-                rim_row >= row,
-                wide(cuts[slice_no, slot, 0, part]),
-                wide(cuts[slice_no, slot, 2, part]),
+            wide(
+                jnp.where(
+                    rim_row >= row,
+                    cuts[slice_no, slot, 0, part],
+                    cuts[slice_no, slot, 2, part],
+                )
             )
         )
         middle = to_left(wide(cuts[slice_no, slot, 1, part]))
@@ -293,13 +294,9 @@
                     part * SIDE : (part + 1) * SIDE, k * SIDE : (k + 1) * SIDE
                 ].astype(jnp.bfloat16)
 
-    def all_rows(matrix):
-        every = rows[...].reshape(CAP * SIDE, 2 * SIDE)
-        result = jnp.dot(every, matrix[...], preferred_element_type=jnp.float32)
-        waves[...] = result.reshape(CAP, SIDE, 2 * SIDE)
-
-    def from_rows(slot):
-        return waves[slot, :, :SIDE], waves[slot, :, SIDE:]
+    def from_rows(slot, matrix):
+        result = jnp.dot(rows[slot], matrix[...], preferred_element_type=jnp.float32)
+        return result[:, :SIDE], result[:, SIDE:]
 
     def rounded(wave):
         return tuple(wide(plane.astype(jnp.bfloat16)) for plane in wave)
@@ -319,30 +316,26 @@
             matrix_copies[0].wait()
         to_columns(slot, phi, prop_ref)
     matrix_copies[1].wait()
-    all_rows(prop_t_ref)
     for slot in range(CAP):
         for part in range(2):
             object_1[slot, part] = cut(1, slot, part).astype(jnp.bfloat16)
-        wave = from_rows(slot)
+        wave = from_rows(slot, prop_t_ref)
         for part in range(2):
             psi_1[slot, part] = wave[part].astype(jnp.bfloat16)
         phi = product(*rounded(wave), *held_pair(object_1, slot))
         to_columns(slot, phi, dft_ref)
     observed_copy.wait()
-    all_rows(dft_t_ref)
-    for slot in range(CAP):
-        far_re, far_im = from_rows(slot)
+    for slot in range(CAP):
+        far_re, far_im = from_rows(slot, dft_t_ref)
         live = (slot < counts_ref[mine]).astype(jnp.float32)
         misfit = live * (far_re * far_re + far_im * far_im - observed[slot])
         to_columns(slot, (misfit * far_re, misfit * far_im), dft_t_ref)
-    all_rows(dft_ref)
-    for slot in range(CAP):
-        spread = rounded(from_rows(slot))
+    for slot in range(CAP):
+        spread = rounded(from_rows(slot, dft_ref))
         to_columns(slot, conj_product(*held_pair(object_1, slot), *spread), prop_t_ref)
         add_patch(1, slot, conj_product(*held_pair(psi_1, slot), *spread))
-    all_rows(prop_ref)
-    for slot in range(CAP):
-        spread = rounded(from_rows(slot))
+    for slot in range(CAP):
+        spread = rounded(from_rows(slot, prop_ref))
         add_patch(0, slot, conj_product(*psi_0(), *spread))
 
     def narrow(slice_no, first_row):
@@ -366,7 +359,7 @@
     return pl.pallas_call(
         probes_kernel,
         out_shape=[jax.ShapeDtypeStruct((2, M, LW), jnp.float32)] + [rim] * 5,
-        in_specs=[smem] * 3 + [vmem] * 6 + [apart, vmem, apart, apart],
+        in_specs=[smem] * 3 + [apart] * 7 + [vmem, apart, apart],
         out_specs=[vmem] * 6,
         scratch_shapes=[
             pltpu.VMEM((2, CAP, 3, 2, M, WIDE), jnp.bfloat16),
@@ -377,7 +370,6 @@
             pltpu.VMEM((2 * SIDE, CAP * SIDE), jnp.bfloat16),
             pltpu.VMEM((CAP, SIDE, 2 * SIDE), jnp.bfloat16),
             pltpu.VMEM((2, 2, 3 * M, LW), jnp.float32),
-            pltpu.VMEM((CAP, SIDE, 2 * SIDE), jnp.float32),
             pltpu.VMEM((2, 2, 2 * SIDE, 2 * SIDE), jnp.bfloat16),
             pltpu.SemaphoreType.DMA((2, CAP, 3)),
             pltpu.SemaphoreType.DMA,

time: 92.6 us -> 89.6 us (0.968)
  Pallas kernels: 18.9 us -> 16 us
    pallas_call x1, Pallas kernels: 15.8 us -> 12.9 us  [probes(): pl.pallas_call(probes_kernel, out_shape=[jax.ShapeDtypeStruct((2, M, LW),...]
where the time goes in v4:
time: 89.6 us; the launch traced here: 89.4 us
  waiting for transfers between devices  53.1 us (59%)
  Pallas kernels  16 us (18%)
  starting transfers between devices  14.8 us (17%)
  local copies, waits for them, and re-layouts  2.92 us (3%)
  other arithmetic  2.26 us (3%)
    ppermute x2, waiting for transfers between devices, swap_far(): return lax.ppermute(value, 'tile', pairs + [(b, a) for a, b in pairs])  25.4 us
    ppermute x2, waiting for transfers between devices, swap_near(): return lax.ppermute(value, 'tile', [(t, t ^ 1) for t in range(count)])  21.6 us
    ppermute x2, starting transfers between devices, swap_far(): return lax.ppermute(value, 'tile', pairs + [(b, a) for a, b in pairs])  13.3 us
    pallas_call x1, Pallas kernels, probes(): pl.pallas_call(probes_kernel, out_shape=[jax.ShapeDtypeStruct((2, M, LW),...  12.9 us
    ppermute x6, waiting for transfers between devices, across(): return lax.ppermute(value, 'depth', [(0, 1), (1, 0)])  6.05 us
  transfers between devices with their start and end apart: 10, of which 5 were waited for; matrix products, arithmetic and copies ran while one was open for 5% of the time, Pallas kernels for 0%

profile of v4, /device:TPU:128, one launch (start us, length us, event | category | flops | bytes accessed | tf_op | source)
XLA Modules:
  0.0 89.4 jit_solution(10791418138682626392)
XLA Ops:
  0.0 0.0 copy-start.4
  0.0 0.0 copy-start.6
  0.0 1.7 %split_planes.1.own_ref = bf16[2,128,2048]{2,1,0:T(8,128)(2,1)S(1)} custom-call(f32[128,32,128]{2,1,0:T(8,128)} %bitcast.31), custom_call_target="tpu_custom_call" | custom-call | tf_op jit(solution)/shard_map/split_planes/pallas_call | solution.py:78
  1.7 0.0 copy-start.5
  1.7 6.8 %collective-permute-start.3 = (bf16[2,128,2048]{2,1,0:T(8,128)(2,1)S(1)}, bf16[2,128,2048]{2,1,0:T(8,128)(2,1)}, u32[]{:S(2)}, u32[]{:S(2)}) collective-permute-start(bf16[2,128,2048]{2,1,0:T(8,128)(2,1)S(1)} %split_planes.1.own_ref), channel_id=1, source_target_pairs={{1,2},{3,4},{5,6},{7,8},{9,10},{11,12},{13,14},{15,16},{17,18},{19... | collective-permute-start | bytes 3145736 | tf_op jit(solution)/shard_map/ppermute | solution.py:391
  8.5 0.1 collective-permute-start.1
  8.6 0.1 collective-permute-start
  8.7 0.0 copy-done.4
  8.7 0.4 fusion.2
  9.1 0.1 copy.20
  9.3 0.0 copy-done.6
  9.3 0.1 reshape.13
  9.4 0.1 copy.19
  9.5 0.9 fusion.1
  10.4 1.0 %copy.13 = bf16[1,512,512]{2,1,0:T(8,128)(2,1)} copy(bf16[1,512,512]{1,2,0:T(8,128)(2,1)S(1)} %get-tuple-element.37) | data formatting | bytes 1048576 | tf_op jit(solution)/shard_map/stack | solution.py:408
  11.4 0.0 copy-start.2
  11.4 0.0 copy-start.3
  11.4 0.1 pad_add_fusion.device_ref
  11.5 0.0 copy-done.5
  11.5 0.0 copy-start
  11.5 0.0 copy-start.1
  11.5 0.4 fusion.3
  11.9 0.5 copy-done.2
  12.4 0.2 copy-done.3
  12.6 0.1 pad_maximum_fusion.prop_hbm
  12.7 21.6 %collective-permute-done.near_ref = bf16[2,128,2048]{2,1,0:T(8,128)(2,1)} collective-permute-done((bf16[2,128,2048]{2,1,0:T(8,128)(2,1)S(1)}, bf16[2,128,2048]{2,1,0:T(8,128)(2,1)}, u32[]{:S(2)}, u32[]{:S(2)}) %collective-permute-start) | collective-permute-done | bytes 1048608 | tf_op jit(solution)/shard_map/ppermute | solution.py:385
  34.3 0.0 collective-permute-done.3.far_ref
  34.3 0.0 collective-permute-start.4
  34.3 0.5 collective-permute-start.2
  34.8 0.1 copy.15.places_ref
  34.9 0.0 collective-permute-done.1.own_o_ref
  34.9 2.4 %collective-permute-done.4.far_o_ref = bf16[2,128,2048]{2,1,0:T(8,128)(2,1)} collective-permute-done((bf16[2,128,2048]{2,1,0:T(8,128)(2,1)}, bf16[2,128,2048]{2,1,0:T(8,128)(2,1)}, u32[]{:S(2)}, u32[]{:S(2)}) %collective-permute-start.4) | collective-permute-done | bytes 1048608 | tf_op jit(solution)/shard_map/ppermute | solution.py:395
  37.3 1.5 %collective-permute-done.2.near_o_ref = bf16[2,128,2048]{2,1,0:T(8,128)(2,1)} collective-permute-done((bf16[2,128,2048]{2,1,0:T(8,128)(2,1)}, bf16[2,128,2048]{2,1,0:T(8,128)(2,1)}, u32[]{:S(2)}, u32[]{:S(2)}) %collective-permute-start.2) | collective-permute-done | bytes 1048608 | tf_op jit(solution)/shard_map/ppermute | solution.py:395
  38.8 0.0 copy-done
  38.8 0.0 copy-done.1
  38.8 12.9 %probes.1 = (f32[2,128,2048]{2,1,0:T(8,128)S(1)}, bf16[2,128,2048]{2,1,0:T(8,128)(2,1)S(1)}, bf16[2,128,2048]{2,1,0:T(8,128)(2,1)S(1)}, bf16[2,128,2048]{2,1,0:T...) custom-call(s32[2]{0:T(128)S(1)} %pad_add_fusion.device_ref, ...), custom_call_target="tpu_custom_call" | custom-call | tf_op jit(solution)/shard_map/probes/pallas_call | solution.py:359
  51.7 0.2 collective-permute-start.5
  52.0 0.4 collective-permute-start.6
  52.3 2.1 %collective-permute-done.5 = bf16[2,128,2048]{2,1,0:T(8,128)(2,1)S(1)} collective-permute-done((bf16[2,128,2048]{2,1,0:T(8,128)(2,1)S(1)}, bf16[2,128,2048]{2,1,0:T(8,128)(2,1)S(1)}, u32[]{:S(2)}, u32[]{:S(2)}) %collective-permute-start.5) | collective-permute-done | bytes 1048608 | tf_op jit(solution)/shard_map/ppermute | solution.py:395
  54.5 0.4 add.17
  54.9 6.5 %collective-permute-start.8 = (bf16[2,128,2048]{2,1,0:T(8,128)(2,1)S(1)}, bf16[2,128,2048]{2,1,0:T(8,128)(2,1)S(1)}, u32[]{:S(2)}, u32[]{:S(2)}) collective-permute-start(bf16[2,128,2048]{2,1,0:T(8,128)(2,1)S(1)} %add.17), channel_id=1, source_target_pairs={{1,2},{3,4},{5,6},{7,8},{9,10},{11,12},{13,14},{15,16},{17,18},{19... | collective-permute-start | bytes 3145736 | tf_op jit(solution)/shard_map/ppermute | solution.py:391
  61.4 0.0 collective-permute-done.6
  61.4 0.1 collective-permute-start.7
  61.5 0.4 add.20
  61.9 0.1 collective-permute-start.9
  62.0 25.4 %collective-permute-done.8 = bf16[2,128,2048]{2,1,0:T(8,128)(2,1)S(1)} collective-permute-done((bf16[2,128,2048]{2,1,0:T(8,128)(2,1)S(1)}, bf16[2,128,2048]{2,1,0:T(8,128)(2,1)S(1)}, u32[]{:S(2)}, u32[]{:S(2)}) %collective-permute-start.8) | collective-permute-done | bytes 1048608 | tf_op jit(solution)/shard_map/ppermute | solution.py:391
  87.4 0.0 collective-permute-done.7
  87.4 0.4 convert_add_fusion.inner_ref
  87.8 0.0 collective-permute-done.9.far_ref
  87.8 1.4 %add_up.1 = f32[128,32,128]{2,1,0:T(8,128)} custom-call(f32[2,128,2048]{2,1,0:T(8,128)S(1)} %convert_add_fusion.inner_ref, bf16[2,128,2048]{2,1,0:T(8,128)(2,1)S(1)} %collective-permute-done.9.far_ref), custom_call_target="tpu_custom_call" | custom-call | tf_op jit(solution)/shard_map/add_up/pallas_call | solution.py:115
  (4 shorter events, 0.1 us)
Async XLA Ops:
  0.0 8.7 %copy-start.4 = (bf16[256,2,256]{2,1,0:T(2,128)(2,1)S(1)}, bf16[256,2,256]{2,1,0:T(2,128)(2,1)}, u32[]{:S(2)}) copy-start(bf16[256,2,256]{2,1,0:T(2,128)(2,1)} %param.9) | copy-start | bytes 786436
  0.0 9.3 %copy-start.6 = (s32[1,2,5,2]{2,3,1,0:T(2,128)S(1)}, s32[1,2,5,2]{2,3,1,0:T(2,128)}, u32[]{:S(2)}) copy-start(s32[1,2,5,2]{2,3,1,0:T(2,128)} %param.10) | copy-start | bytes 244
  1.7 9.8 %copy-start.5 = (bf16[256,2,256]{2,1,0:T(2,128)(2,1)S(1)}, bf16[256,2,256]{2,1,0:T(2,128)(2,1)}, u32[]{:S(2)}) copy-start(bf16[256,2,256]{2,1,0:T(2,128)(2,1)} %param.8) | copy-start | bytes 786436
  1.7 32.6 %collective-permute-start.3 = (bf16[2,128,2048]{2,1,0:T(8,128)(2,1)S(1)}, bf16[2,128,2048]{2,1,0:T(8,128)(2,1)}, u32[]{:S(2)}, u32[]{:S(2)}) collective-permute-start(bf16[2,128,2048]{2,1,0:T(8,128)(2,1)S(1)} %split_planes.1.own_ref), channel_id=1, source_target_pairs={{1,2},{3,4},{5,6},{7,8},{9,10},{11,12},{13,14},{15,16},{17,18},{19... | collective-permute-start | bytes 3145736 | tf_op jit(solution)/shard_map/ppermute | solution.py:391
  8.5 26.4 %collective-permute-start.1 = (bf16[2,128,2048]{2,1,0:T(8,128)(2,1)S(1)}, bf16[2,128,2048]{2,1,0:T(8,128)(2,1)}, u32[]{:S(2)}, u32[]{:S(2)}) collective-permute-start(bf16[2,128,2048]{2,1,0:T(8,128)(2,1)S(1)} %split_planes.1.own_ref), channel_id=1, source_target_pairs={{0,128},{128,0},{1,129},{129,1},{2,130},{130,2},{3,131},{131,3},{4... | collective-permute-start | bytes 3145736 | tf_op jit(solution)/shard_map/ppermute | solution.py:395
  8.6 25.7 %collective-permute-start = (bf16[2,128,2048]{2,1,0:T(8,128)(2,1)S(1)}, bf16[2,128,2048]{2,1,0:T(8,128)(2,1)}, u32[]{:S(2)}, u32[]{:S(2)}) collective-permute-start(bf16[2,128,2048]{2,1,0:T(8,128)(2,1)S(1)} %split_planes.1.own_ref), channel_id=1, source_target_pairs={{0,1},{1,0},{2,3},{3,2},{4,5},{5,4},{6,7},{7,6},{8,9},{9,8},{10,11... | collective-permute-start | bytes 3145736 | tf_op jit(solution)/shard_map/ppermute | solution.py:385
  11.4 1.0 %copy-start.2 = (bf16[1,512,512]{2,1,0:T(8,128)(2,1)S(1)}, bf16[1,512,512]{2,1,0:T(8,128)(2,1)}, u32[]{:S(2)}) copy-start(bf16[1,512,512]{2,1,0:T(8,128)(2,1)} %copy.13) | copy-start | bytes 1572868
  11.4 1.2 %copy-start.3 = (bf16[1,512,512]{2,1,0:T(8,128)(2,1)S(1)}, bf16[1,512,512]{2,1,0:T(8,128)(2,1)}, u32[]{:S(2)}) copy-start(bf16[1,512,512]{2,1,0:T(8,128)(2,1)} %get-tuple-element.38) | copy-start | bytes 1572868
  11.5 27.3 %copy-start = (bf16[2,512,512]{2,1,0:T(8,128)(2,1)S(1)}, bf16[2,512,512]{2,1,0:T(8,128)(2,1)}, u32[]{:S(2)}) copy-start(bf16[2,512,512]{2,1,0:T(8,128)(2,1)} %constant.24.clone.dft_hbm) | copy-start | bytes 3145732
  11.5 27.3 %copy-start.1 = (s32[1,2]{1,0:T(1,128)S(1)}, s32[1,2]{1,0:T(1,128)}, u32[]{:S(2)}) copy-start(s32[1,2]{1,0:T(1,128)} %param.11) | copy-start | bytes 28
  34.3 3.0 %collective-permute-start.4 = (bf16[2,128,2048]{2,1,0:T(8,128)(2,1)}, bf16[2,128,2048]{2,1,0:T(8,128)(2,1)}, u32[]{:S(2)}, u32[]{:S(2)}) collective-permute-start(bf16[2,128,2048]{2,1,0:T(8,128)(2,1)} %collective-permute-done.3.far_ref), channel_id=1, source_target_pairs={{0,128},{128,0},{1,129},{129,1},{2,130},{130,2},{3,131},{131,3},{4... | collective-permute-start | bytes 3145736 | tf_op jit(solution)/shard_map/ppermute | solution.py:395
  34.3 4.5 %collective-permute-start.2 = (bf16[2,128,2048]{2,1,0:T(8,128)(2,1)}, bf16[2,128,2048]{2,1,0:T(8,128)(2,1)}, u32[]{:S(2)}, u32[]{:S(2)}) collective-permute-start(bf16[2,128,2048]{2,1,0:T(8,128)(2,1)} %collective-permute-done.near_ref), channel_id=1, source_target_pairs={{0,128},{128,0},{1,129},{129,1},{2,130},{130,2},{3,131},{131,3},{4... | collective-permute-start | bytes 3145736 | tf_op jit(solution)/shard_map/ppermute | solution.py:395
  51.7 2.7 %collective-permute-start.5 = (bf16[2,128,2048]{2,1,0:T(8,128)(2,1)S(1)}, bf16[2,128,2048]{2,1,0:T(8,128)(2,1)S(1)}, u32[]{:S(2)}, u32[]{:S(2)}) collective-permute-start(bf16[2,128,2048]{2,1,0:T(8,128)(2,1)S(1)} %get-tuple-element.29), channel_id=1, source_target_pairs={{0,128},{128,0},{1,129},{129,1},{2,130},{130,2},{3,131},{131,3},{4... | collective-permute-start | bytes 3145736 | tf_op jit(solution)/shard_map/ppermute | solution.py:395
  52.0 9.4 %collective-permute-start.6 = (bf16[2,128,2048]{2,1,0:T(8,128)(2,1)S(1)}, bf16[2,128,2048]{2,1,0:T(8,128)(2,1)S(1)}, u32[]{:S(2)}, u32[]{:S(2)}) collective-permute-start(bf16[2,128,2048]{2,1,0:T(8,128)(2,1)S(1)} %get-tuple-element.30), channel_id=1, source_target_pairs={{0,128},{128,0},{1,129},{129,1},{2,130},{130,2},{3,131},{131,3},{4... | collective-permute-start | bytes 3145736 | tf_op jit(solution)/shard_map/ppermute | solution.py:395
  54.9 32.5 %collective-permute-start.8 = (bf16[2,128,2048]{2,1,0:T(8,128)(2,1)S(1)}, bf16[2,128,2048]{2,1,0:T(8,128)(2,1)S(1)}, u32[]{:S(2)}, u32[]{:S(2)}) collective-permute-start(bf16[2,128,2048]{2,1,0:T(8,128)(2,1)S(1)} %add.17), channel_id=1, source_target_pairs={{1,2},{3,4},{5,6},{7,8},{9,10},{11,12},{13,14},{15,16},{17,18},{19... | collective-permute-start | bytes 3145736 | tf_op jit(solution)/shard_map/ppermute | solution.py:391
  61.4 26.0 %collective-permute-start.7 = (bf16[2,128,2048]{2,1,0:T(8,128)(2,1)S(1)}, bf16[2,128,2048]{2,1,0:T(8,128)(2,1)S(1)}, u32[]{:S(2)}, u32[]{:S(2)}) collective-permute-start(bf16[2,128,2048]{2,1,0:T(8,128)(2,1)S(1)} %get-tuple-element.32), channel_id=1, source_target_pairs={{0,128},{128,0},{1,129},{129,1},{2,130},{130,2},{3,131},{131,3},{4... | collective-permute-start | bytes 3145736 | tf_op jit(solution)/shard_map/ppermute | solution.py:395
  61.9 25.9 %collective-permute-start.9 = (bf16[2,128,2048]{2,1,0:T(8,128)(2,1)S(1)}, bf16[2,128,2048]{2,1,0:T(8,128)(2,1)S(1)}, u32[]{:S(2)}, u32[]{:S(2)}) collective-permute-start(bf16[2,128,2048]{2,1,0:T(8,128)(2,1)S(1)} %add.20), channel_id=1, source_target_pairs={{0,1},{1,0},{2,3},{3,2},{4,5},{5,4},{6,7},{7,6},{8,9},{9,8},{10,11... | collective-permute-start | bytes 3145736 | tf_op jit(solution)/shard_map/ppermute | solution.py:385

commit v5 on v4

--- a/solution.py
+++ b/solution.py
@@ -47,7 +47,7 @@
 
 LINES = 2 * BLOCKS
 PITCH = LINES + GROUP
-STEPS = 4
+STEPS = 8
 ROWS = M // STEPS
 
 

time: 89.6 us -> 89.6 us (level)
  no operation moved by 1% of the time
where the time goes in v5:
time: 89.6 us; the launch traced here: 89.4 us
  waiting for transfers between devices  53.3 us (59%)
  Pallas kernels  15.9 us (18%)
  starting transfers between devices  14.6 us (16%)
  local copies, waits for them, and re-layouts  2.92 us (3%)
  other arithmetic  2.25 us (3%)
    ppermute x2, waiting for transfers between devices, swap_far(): return lax.ppermute(value, 'tile', pairs + [(b, a) for a, b in pairs])  25.6 us
    ppermute x2, waiting for transfers between devices, swap_near(): return lax.ppermute(value, 'tile', [(t, t ^ 1) for t in range(count)])  21.6 us
    ppermute x2, starting transfers between devices, swap_far(): return lax.ppermute(value, 'tile', pairs + [(b, a) for a, b in pairs])  13.1 us
    pallas_call x1, Pallas kernels, probes(): pl.pallas_call(probes_kernel, out_shape=[jax.ShapeDtypeStruct((2, M, LW),...  12.9 us
    ppermute x6, waiting for transfers between devices, across(): return lax.ppermute(value, 'depth', [(0, 1), (1, 0)])  6.05 us
  transfers between devices with their start and end apart: 10, of which 5 were waited for; matrix products, arithmetic and copies ran while one was open for 5% of the time, Pallas kernels for 0%

profile of v5, /device:TPU:128, one launch (start us, length us, event | category | flops | bytes accessed | tf_op | source)
XLA Modules:
  0.0 89.4 jit_solution(242946111827463853)
XLA Ops:
  0.0 0.0 copy-start.4
  0.0 0.0 copy-start.6
  0.0 1.7 %split_planes.1.own_ref = bf16[2,128,2048]{2,1,0:T(8,128)(2,1)S(1)} custom-call(f32[128,32,128]{2,1,0:T(8,128)} %bitcast.31), custom_call_target="tpu_custom_call" | custom-call | tf_op jit(solution)/shard_map/split_planes/pallas_call | solution.py:78
  1.7 0.0 copy-start.5
  1.7 6.8 %collective-permute-start.3 = (bf16[2,128,2048]{2,1,0:T(8,128)(2,1)S(1)}, bf16[2,128,2048]{2,1,0:T(8,128)(2,1)}, u32[]{:S(2)}, u32[]{:S(2)}) collective-permute-start(bf16[2,128,2048]{2,1,0:T(8,128)(2,1)S(1)} %split_planes.1.own_ref), channel_id=1, source_target_pairs={{1,2},{3,4},{5,6},{7,8},{9,10},{11,12},{13,14},{15,16},{17,18},{19... | collective-permute-start | bytes 3145736 | tf_op jit(solution)/shard_map/ppermute | solution.py:391
  8.5 0.1 collective-permute-start.1
  8.6 0.1 collective-permute-start
  8.7 0.0 copy-done.4
  8.7 0.4 fusion.2
  9.1 0.1 copy.20
  9.3 0.0 copy-done.6
  9.3 0.1 reshape.13
  9.4 0.1 copy.19
  9.5 0.9 fusion.1
  10.4 1.0 %copy.13 = bf16[1,512,512]{2,1,0:T(8,128)(2,1)} copy(bf16[1,512,512]{1,2,0:T(8,128)(2,1)S(1)} %get-tuple-element.37) | data formatting | bytes 1048576 | tf_op jit(solution)/shard_map/stack | solution.py:408
  11.4 0.0 copy-start.2
  11.4 0.0 copy-start.3
  11.4 0.1 pad_add_fusion.device_ref
  11.4 0.0 copy-done.5
  11.4 0.0 copy-start
  11.4 0.0 copy-start.1
  11.5 0.4 fusion.3
  11.9 0.5 copy-done.2
  12.4 0.2 copy-done.3
  12.6 0.1 pad_maximum_fusion.prop_hbm
  12.7 21.6 %collective-permute-done.near_ref = bf16[2,128,2048]{2,1,0:T(8,128)(2,1)} collective-permute-done((bf16[2,128,2048]{2,1,0:T(8,128)(2,1)S(1)}, bf16[2,128,2048]{2,1,0:T(8,128)(2,1)}, u32[]{:S(2)}, u32[]{:S(2)}) %collective-permute-start) | collective-permute-done | bytes 1048608 | tf_op jit(solution)/shard_map/ppermute | solution.py:385
  34.3 0.0 collective-permute-done.3.far_ref
  34.3 0.0 collective-permute-start.4
  34.3 0.5 collective-permute-start.2
  34.8 0.1 copy.15.places_ref
  34.9 0.0 collective-permute-done.1.own_o_ref
  34.9 2.4 %collective-permute-done.4.far_o_ref = bf16[2,128,2048]{2,1,0:T(8,128)(2,1)} collective-permute-done((bf16[2,128,2048]{2,1,0:T(8,128)(2,1)}, bf16[2,128,2048]{2,1,0:T(8,128)(2,1)}, u32[]{:S(2)}, u32[]{:S(2)}) %collective-permute-start.4) | collective-permute-done | bytes 1048608 | tf_op jit(solution)/shard_map/ppermute | solution.py:395
  37.3 1.5 %collective-permute-done.2.near_o_ref = bf16[2,128,2048]{2,1,0:T(8,128)(2,1)} collective-permute-done((bf16[2,128,2048]{2,1,0:T(8,128)(2,1)}, bf16[2,128,2048]{2,1,0:T(8,128)(2,1)}, u32[]{:S(2)}, u32[]{:S(2)}) %collective-permute-start.2) | collective-permute-done | bytes 1048608 | tf_op jit(solution)/shard_map/ppermute | solution.py:395
  38.8 0.0 copy-done
  38.8 0.0 copy-done.1
  38.8 12.9 %probes.1 = (f32[2,128,2048]{2,1,0:T(8,128)S(1)}, bf16[2,128,2048]{2,1,0:T(8,128)(2,1)S(1)}, bf16[2,128,2048]{2,1,0:T(8,128)(2,1)S(1)}, bf16[2,128,2048]{2,1,0:T...) custom-call(s32[2]{0:T(128)S(1)} %pad_add_fusion.device_ref, ...), custom_call_target="tpu_custom_call" | custom-call | tf_op jit(solution)/shard_map/probes/pallas_call | solution.py:359
  51.7 0.1 collective-permute-start.5
  51.8 0.5 collective-permute-start.6
  52.3 2.1 %collective-permute-done.5 = bf16[2,128,2048]{2,1,0:T(8,128)(2,1)S(1)} collective-permute-done((bf16[2,128,2048]{2,1,0:T(8,128)(2,1)S(1)}, bf16[2,128,2048]{2,1,0:T(8,128)(2,1)S(1)}, u32[]{:S(2)}, u32[]{:S(2)}) %collective-permute-start.5) | collective-permute-done | bytes 1048608 | tf_op jit(solution)/shard_map/ppermute | solution.py:395
  54.4 0.4 add.17
  54.8 6.3 %collective-permute-start.8 = (bf16[2,128,2048]{2,1,0:T(8,128)(2,1)S(1)}, bf16[2,128,2048]{2,1,0:T(8,128)(2,1)S(1)}, u32[]{:S(2)}, u32[]{:S(2)}) collective-permute-start(bf16[2,128,2048]{2,1,0:T(8,128)(2,1)S(1)} %add.17), channel_id=1, source_target_pairs={{1,2},{3,4},{5,6},{7,8},{9,10},{11,12},{13,14},{15,16},{17,18},{19... | collective-permute-start | bytes 3145736 | tf_op jit(solution)/shard_map/ppermute | solution.py:391
  61.1 0.0 collective-permute-done.6
  61.1 0.1 collective-permute-start.7
  61.2 0.4 add.20
  61.6 0.1 collective-permute-start.9
  61.7 25.6 %collective-permute-done.8 = bf16[2,128,2048]{2,1,0:T(8,128)(2,1)S(1)} collective-permute-done((bf16[2,128,2048]{2,1,0:T(8,128)(2,1)S(1)}, bf16[2,128,2048]{2,1,0:T(8,128)(2,1)S(1)}, u32[]{:S(2)}, u32[]{:S(2)}) %collective-permute-start.8) | collective-permute-done | bytes 1048608 | tf_op jit(solution)/shard_map/ppermute | solution.py:391
  87.3 0.0 collective-permute-done.7
  87.3 0.4 convert_add_fusion.inner_ref
  87.7 0.0 collective-permute-done.9.far_ref
  87.8 1.4 %add_up.1 = f32[128,32,128]{2,1,0:T(8,128)} custom-call(f32[2,128,2048]{2,1,0:T(8,128)S(1)} %convert_add_fusion.inner_ref, bf16[2,128,2048]{2,1,0:T(8,128)(2,1)S(1)} %collective-permute-done.9.far_ref), custom_call_target="tpu_custom_call" | custom-call | tf_op jit(solution)/shard_map/add_up/pallas_call | solution.py:115
  (4 shorter events, 0.1 us)
Async XLA Ops:
  0.0 8.7 %copy-start.4 = (bf16[256,2,256]{2,1,0:T(2,128)(2,1)S(1)}, bf16[256,2,256]{2,1,0:T(2,128)(2,1)}, u32[]{:S(2)}) copy-start(bf16[256,2,256]{2,1,0:T(2,128)(2,1)} %param.9) | copy-start | bytes 786436
  0.0 9.3 %copy-start.6 = (s32[1,2,5,2]{2,3,1,0:T(2,128)S(1)}, s32[1,2,5,2]{2,3,1,0:T(2,128)}, u32[]{:S(2)}) copy-start(s32[1,2,5,2]{2,3,1,0:T(2,128)} %param.10) | copy-start | bytes 244
  1.7 9.8 %copy-start.5 = (bf16[256,2,256]{2,1,0:T(2,128)(2,1)S(1)}, bf16[256,2,256]{2,1,0:T(2,128)(2,1)}, u32[]{:S(2)}) copy-start(bf16[256,2,256]{2,1,0:T(2,128)(2,1)} %param.8) | copy-start | bytes 786436
  1.7 32.6 %collective-permute-start.3 = (bf16[2,128,2048]{2,1,0:T(8,128)(2,1)S(1)}, bf16[2,128,2048]{2,1,0:T(8,128)(2,1)}, u32[]{:S(2)}, u32[]{:S(2)}) collective-permute-start(bf16[2,128,2048]{2,1,0:T(8,128)(2,1)S(1)} %split_planes.1.own_ref), channel_id=1, source_target_pairs={{1,2},{3,4},{5,6},{7,8},{9,10},{11,12},{13,14},{15,16},{17,18},{19... | collective-permute-start | bytes 3145736 | tf_op jit(solution)/shard_map/ppermute | solution.py:391
  8.5 26.4 %collective-permute-start.1 = (bf16[2,128,2048]{2,1,0:T(8,128)(2,1)S(1)}, bf16[2,128,2048]{2,1,0:T(8,128)(2,1)}, u32[]{:S(2)}, u32[]{:S(2)}) collective-permute-start(bf16[2,128,2048]{2,1,0:T(8,128)(2,1)S(1)} %split_planes.1.own_ref), channel_id=1, source_target_pairs={{0,128},{128,0},{1,129},{129,1},{2,130},{130,2},{3,131},{131,3},{4... | collective-permute-start | bytes 3145736 | tf_op jit(solution)/shard_map/ppermute | solution.py:395
  8.6 25.7 %collective-permute-start = (bf16[2,128,2048]{2,1,0:T(8,128)(2,1)S(1)}, bf16[2,128,2048]{2,1,0:T(8,128)(2,1)}, u32[]{:S(2)}, u32[]{:S(2)}) collective-permute-start(bf16[2,128,2048]{2,1,0:T(8,128)(2,1)S(1)} %split_planes.1.own_ref), channel_id=1, source_target_pairs={{0,1},{1,0},{2,3},{3,2},{4,5},{5,4},{6,7},{7,6},{8,9},{9,8},{10,11... | collective-permute-start | bytes 3145736 | tf_op jit(solution)/shard_map/ppermute | solution.py:385
  11.4 1.0 %copy-start.2 = (bf16[1,512,512]{2,1,0:T(8,128)(2,1)S(1)}, bf16[1,512,512]{2,1,0:T(8,128)(2,1)}, u32[]{:S(2)}) copy-start(bf16[1,512,512]{2,1,0:T(8,128)(2,1)} %copy.13) | copy-start | bytes 1572868
  11.4 1.2 %copy-start.3 = (bf16[1,512,512]{2,1,0:T(8,128)(2,1)S(1)}, bf16[1,512,512]{2,1,0:T(8,128)(2,1)}, u32[]{:S(2)}) copy-start(bf16[1,512,512]{2,1,0:T(8,128)(2,1)} %get-tuple-element.38) | copy-start | bytes 1572868
  11.4 27.3 %copy-start = (bf16[2,512,512]{2,1,0:T(8,128)(2,1)S(1)}, bf16[2,512,512]{2,1,0:T(8,128)(2,1)}, u32[]{:S(2)}) copy-start(bf16[2,512,512]{2,1,0:T(8,128)(2,1)} %constant.24.clone.dft_hbm) | copy-start | bytes 3145732
  11.4 27.3 %copy-start.1 = (s32[1,2]{1,0:T(1,128)S(1)}, s32[1,2]{1,0:T(1,128)}, u32[]{:S(2)}) copy-start(s32[1,2]{1,0:T(1,128)} %param.11) | copy-start | bytes 28
  34.3 3.0 %collective-permute-start.4 = (bf16[2,128,2048]{2,1,0:T(8,128)(2,1)}, bf16[2,128,2048]{2,1,0:T(8,128)(2,1)}, u32[]{:S(2)}, u32[]{:S(2)}) collective-permute-start(bf16[2,128,2048]{2,1,0:T(8,128)(2,1)} %collective-permute-done.3.far_ref), channel_id=1, source_target_pairs={{0,128},{128,0},{1,129},{129,1},{2,130},{130,2},{3,131},{131,3},{4... | collective-permute-start | bytes 3145736 | tf_op jit(solution)/shard_map/ppermute | solution.py:395
  34.3 4.5 %collective-permute-start.2 = (bf16[2,128,2048]{2,1,0:T(8,128)(2,1)}, bf16[2,128,2048]{2,1,0:T(8,128)(2,1)}, u32[]{:S(2)}, u32[]{:S(2)}) collective-permute-start(bf16[2,128,2048]{2,1,0:T(8,128)(2,1)} %collective-permute-done.near_ref), channel_id=1, source_target_pairs={{0,128},{128,0},{1,129},{129,1},{2,130},{130,2},{3,131},{131,3},{4... | collective-permute-start | bytes 3145736 | tf_op jit(solution)/shard_map/ppermute | solution.py:395
  51.7 2.7 %collective-permute-start.5 = (bf16[2,128,2048]{2,1,0:T(8,128)(2,1)S(1)}, bf16[2,128,2048]{2,1,0:T(8,128)(2,1)S(1)}, u32[]{:S(2)}, u32[]{:S(2)}) collective-permute-start(bf16[2,128,2048]{2,1,0:T(8,128)(2,1)S(1)} %get-tuple-element.29), channel_id=1, source_target_pairs={{0,128},{128,0},{1,129},{129,1},{2,130},{130,2},{3,131},{131,3},{4... | collective-permute-start | bytes 3145736 | tf_op jit(solution)/shard_map/ppermute | solution.py:395
  51.8 9.4 %collective-permute-start.6 = (bf16[2,128,2048]{2,1,0:T(8,128)(2,1)S(1)}, bf16[2,128,2048]{2,1,0:T(8,128)(2,1)S(1)}, u32[]{:S(2)}, u32[]{:S(2)}) collective-permute-start(bf16[2,128,2048]{2,1,0:T(8,128)(2,1)S(1)} %get-tuple-element.30), channel_id=1, source_target_pairs={{0,128},{128,0},{1,129},{129,1},{2,130},{130,2},{3,131},{131,3},{4... | collective-permute-start | bytes 3145736 | tf_op jit(solution)/shard_map/ppermute | solution.py:395
  54.8 32.5 %collective-permute-start.8 = (bf16[2,128,2048]{2,1,0:T(8,128)(2,1)S(1)}, bf16[2,128,2048]{2,1,0:T(8,128)(2,1)S(1)}, u32[]{:S(2)}, u32[]{:S(2)}) collective-permute-start(bf16[2,128,2048]{2,1,0:T(8,128)(2,1)S(1)} %add.17), channel_id=1, source_target_pairs={{1,2},{3,4},{5,6},{7,8},{9,10},{11,12},{13,14},{15,16},{17,18},{19... | collective-permute-start | bytes 3145736 | tf_op jit(solution)/shard_map/ppermute | solution.py:391
  61.1 26.2 %collective-permute-start.7 = (bf16[2,128,2048]{2,1,0:T(8,128)(2,1)S(1)}, bf16[2,128,2048]{2,1,0:T(8,128)(2,1)S(1)}, u32[]{:S(2)}, u32[]{:S(2)}) collective-permute-start(bf16[2,128,2048]{2,1,0:T(8,128)(2,1)S(1)} %get-tuple-element.32), channel_id=1, source_target_pairs={{0,128},{128,0},{1,129},{129,1},{2,130},{130,2},{3,131},{131,3},{4... | collective-permute-start | bytes 3145736 | tf_op jit(solution)/shard_map/ppermute | solution.py:395
  61.6 26.1 %collective-permute-start.9 = (bf16[2,128,2048]{2,1,0:T(8,128)(2,1)S(1)}, bf16[2,128,2048]{2,1,0:T(8,128)(2,1)S(1)}, u32[]{:S(2)}, u32[]{:S(2)}) collective-permute-start(bf16[2,128,2048]{2,1,0:T(8,128)(2,1)S(1)} %add.20), channel_id=1, source_target_pairs={{0,1},{1,0},{2,3},{3,2},{4,5},{5,4},{6,7},{7,6},{8,9},{9,8},{10,11... | collective-permute-start | bytes 3145736 | tf_op jit(solution)/shard_map/ppermute | solution.py:385
